TPU v7x, 128 devices: a whole 4x4x4 slice. The times are simulated.
128 devices in a mesh: grp: 8 (over y, core), fsdp: 16 (over x, z).
Axes of the slice: x: 4, y: 4, z: 4, core: 2. Of those that a mesh axis runs over, the one named last changes fastest.
Arguments:
- tokens: bfloat16 [24576, 8192], P(('grp', 'fsdp')), may hold values from -6 to 6
- targets: bfloat16 [24576, 1024], P(('grp', 'fsdp')), may hold values from -6 to 6
- row_owner_user: int32 [24576, 1], P(('grp', 'fsdp')), may hold values from 0 to 127; in each aligned block of 192 rows (0 to 191, 192 to 383, ...) at most 2 rows name the same one
- device_row_count: int32 [128], P(('grp', 'fsdp')), may hold values from 1 to 192, 18432 in all
- user_row_cap: int32 [128], replicated, may hold values from 48 to 383
- value_weight: bfloat16 [8192, 1024], P('fsdp'), may hold values from -0.0625 to 0.0625
- adapter_down: bfloat16 [8192, 64], replicated, may hold values from -0.0625 to 0.0625
- adapter_up: bfloat16 [64, 1024], replicated, may hold values from -0.75 to 0.75
- clip_norm_bound: float32 [1], replicated, may hold values from 2 to 6
- down_noise: float32 [8192, 64], P(('grp', 'fsdp')), may hold values from -0.12 to 0.12
- up_noise: float32 [64, 1024], P(None, ('grp', 'fsdp')), may hold values from -0.12 to 0.12
Outputs:
- update_a: float32 [8192, 64], P(('grp', 'fsdp'))
- update_b: float32 [64, 1024], P(None, ('grp', 'fsdp'))
Inputs may be any that keep to these rules, and one draw needn't show every extreme that they name: `row_owner_user`: within the rows of one device (aligned blocks of 192 rows) no user is named by more than 2 rows, a bound that some block reaches. `device_row_count`: the counts sum to 18432.
All inputs are finite; a program needn't handle non-finite values. No bound on the sum of `device_row_count` on one device may be relied on, other than what follows from the above.
Results may differ from a plain program's by a relative error of at most 0.00084.
Values may be sent and summed in bfloat16 or wider, within the bound.
A program may use at most 128 MiB of HBM per device.

v0:
```python
import jax
import jax.numpy as jnp
from jax import lax
from jax.sharding import PartitionSpec as P

STEPS = 2


adapter_scale = 2.0
learn_rate = 0.05
epsilon = 1e-06


def entering(value, axis, join, neutral):
    count, mine = (lax.axis_size(axis), lax.axis_index(axis))
    pieces = lax.all_gather(value, axis)
    running = jnp.full_like(value, 0) + jnp.asarray(neutral, value.dtype)

    def turn(position, running):
        longer = join(running, pieces[position])
        return jnp.where(position < mine, longer, running)

    return lax.fori_loop(0, count - 1, turn, running)


def adapter_step(
    input_rows,
    frozen_output,
    target_value,
    live_mask,
    capped_value,
    adapter_down,
    adapter_up,
    clipped_value_rows,
):
    current_down = adapter_down.astype(jnp.float32)
    current_up = adapter_up.astype(jnp.float32)
    for repeat in range(STEPS):
        a_half = current_down.astype(jnp.bfloat16)
        half_up_matrix = current_up.astype(jnp.bfloat16)
        hidden_input = jnp.dot(input_rows, a_half, preferred_element_type=jnp.float32).astype(
            jnp.bfloat16
        )
        value_output = frozen_output + adapter_scale * jnp.dot(
            hidden_input, half_up_matrix, preferred_element_type=jnp.float32
        )
        residual_error = (
            live_mask[:, None] * (value_output - target_value.astype(jnp.float32)) / capped_value
        ).astype(jnp.bfloat16)
        up_gradient = adapter_scale * lax.dot_general(
            hidden_input,
            residual_error,
            (((0,), (0,)), ((), ())),
            preferred_element_type=jnp.float32,
        )
        backward_pass = jnp.dot(
            residual_error, half_up_matrix.T, preferred_element_type=jnp.float32
        ).astype(jnp.bfloat16)
        down_gradient = adapter_scale * lax.dot_general(
            input_rows, backward_pass, (((0,), (0,)), ((), ())), preferred_element_type=jnp.float32
        )
        current_down = current_down - learn_rate * down_gradient
        current_up = current_up - learn_rate * up_gradient
    down_delta = current_down - adapter_down.astype(jnp.float32)
    up_delta = current_up - adapter_up.astype(jnp.float32)
    total = jnp.sum(down_delta * down_delta) + jnp.sum(up_delta * up_delta)
    factor = jnp.minimum(1.0, clipped_value_rows / jnp.sqrt(total + epsilon))
    return (factor * down_delta, factor * up_delta)


def add_counts(earlier, later):
    return earlier + later


def body(
    tokens,
    targets,
    row_owner_user,
    device_row_count,
    user_row_cap,
    value_weight,
    adapter_down,
    adapter_up,
    clip_norm_bound,
    down_noise,
    up_noise,
):
    devices = lax.axis_size(("grp", "fsdp"))
    myself = lax.axis_index(("grp", "fsdp"))
    per_dev = tokens.shape[0]
    width = tokens.shape[1]
    kv_width = targets.shape[1]
    users = user_row_cap.shape[0]
    most_rows = 3 * per_dev // (2 * devices)
    slot_count = devices * most_rows
    user_of = row_owner_user[:, 0]
    position = jnp.arange(per_dev, dtype=jnp.int32)
    valid = position < device_row_count[0]
    onehot = (user_of[:, None] == jnp.arange(users, dtype=jnp.int32)[None, :]).astype(jnp.float32)
    lower = (position[None, :] < position[:, None]).astype(jnp.float32)
    valid_hot = onehot * valid[:, None].astype(jnp.float32)
    before_all = jnp.dot(lower, onehot, precision=lax.Precision.HIGHEST)
    before_valid = jnp.dot(lower, valid_hot, precision=lax.Precision.HIGHEST)
    row_rank = jnp.sum(before_all * onehot, axis=1).astype(jnp.int32)
    local_earlier = jnp.sum(before_valid * onehot, axis=1)
    counts = jnp.sum(valid_hot, axis=0).astype(jnp.int32)
    prior = entering(counts, ("grp", "fsdp"), add_counts, jnp.zeros_like(counts))
    earlier = local_earlier + jnp.sum(onehot * prior.astype(jnp.float32)[None, :], axis=1)
    cap_row = jnp.sum(onehot * user_row_cap.astype(jnp.float32)[None, :], axis=1)
    kept = valid & (earlier < cap_row)
    slot_index = jnp.where(kept, user_of * most_rows + row_rank, slot_count)
    send_rows = jnp.zeros((slot_count, width), jnp.bfloat16).at[slot_index].set(tokens, mode="drop")
    send_goal = (
        jnp.zeros((slot_count, kv_width), jnp.bfloat16).at[slot_index].set(targets, mode="drop")
    )
    send_live = (
        jnp.zeros((slot_count,), jnp.bfloat16)
        .at[slot_index]
        .set(jnp.ones((per_dev,), jnp.bfloat16), mode="drop")
    )
    got_rows, got_goal, got_live = (
        lax.all_to_all(
            send_rows.reshape(devices, most_rows, width),
            ("grp", "fsdp"),
            split_axis=0,
            concat_axis=0,
            tiled=True,
        ),
        lax.all_to_all(
            send_goal.reshape(devices, most_rows, kv_width),
            ("grp", "fsdp"),
            split_axis=0,
            concat_axis=0,
            tiled=True,
        ),
        lax.all_to_all(
            send_live.reshape(devices, most_rows),
            ("grp", "fsdp"),
            split_axis=0,
            concat_axis=0,
            tiled=True,
        ),
    )
    input_rows = got_rows.reshape(slot_count, width)
    target_value = got_goal.reshape(slot_count, kv_width)
    live_mask = got_live.reshape(slot_count).astype(jnp.float32)
    frozen_output = jnp.dot(
        input_rows,
        lax.all_gather(value_weight, "fsdp", axis=0, tiled=True),
        preferred_element_type=jnp.float32,
    )
    user_row_limit = jnp.sum(
        jnp.where(jnp.arange(users, dtype=jnp.int32) == myself, user_row_cap, 0)
    ).astype(jnp.float32)
    clipped_value_rows = clip_norm_bound[0]
    down_partial, up_partial = adapter_step(
        input_rows,
        frozen_output,
        target_value,
        live_mask,
        user_row_limit,
        adapter_down,
        adapter_up,
        clipped_value_rows,
    )
    summed_a, summed_b = (
        lax.psum_scatter(down_partial, ("grp", "fsdp"), scatter_dimension=0, tiled=True),
        lax.psum_scatter(up_partial, ("grp", "fsdp"), scatter_dimension=1, tiled=True),
    )
    update_a = summed_a + clipped_value_rows * down_noise
    update_b = summed_b + clipped_value_rows * up_noise
    return (update_a, update_b)


def solution(mesh):
    in_specs = (
        P(("grp", "fsdp"), None),
        P(("grp", "fsdp"), None),
        P(("grp", "fsdp"), None),
        P(("grp", "fsdp")),
        P(),
        P("fsdp", None),
        P(),
        P(),
        P(),
        P(("grp", "fsdp"), None),
        P(None, ("grp", "fsdp")),
    )
    out_specs = (P(("grp", "fsdp"), None), P(None, ("grp", "fsdp")))
    return jax.shard_map(body, mesh=mesh, in_specs=in_specs, out_specs=out_specs, check_vma=False)
```

profile of v0, /device:TPU:0, one launch (start us, length us, event | category | flops | bytes accessed | tf_op | source)
XLA Modules:
  0.0 1019.7 jit_solution(1028396314481917)
XLA Ops:
  7.2 0.7 all-gather.4.cloned.1.call-update
  8.6 0.8 select_reduce_fusion
  9.4 49.3 %all-gather.1 = s32[128,1,128]{2,1,0:T(1,128)S(1)} all-gather(s32[1,1,128]{2,1,0:T(1,128)S(1)} %convert_bitcast_fusion), channel_id=2, replica_groups=mesh['grp'=8,'fsdp'=16] {'grp','fsdp'}, dimensions={0}, use_global_device_ids=true | all-gather | bytes 66048 | tf_op jit(solution)/shard_map/all_gather | solution.py:16
  58.7 5.1 while.14
  63.8 1.1 fusion.19
  64.9 1.4 fusion.31
  66.3 0.9 select_reduce_fusion.2
  67.2 1.2 fusion.18
  68.4 0.7 compare_select_fusion
  69.1 1.8 scatter_custom_fusion.1
  70.8 0.8 all_to_all.16
  71.6 7.2 all-to-all-start.1
  78.9 2.0 scatter_custom_fusion.2
  80.9 1.0 reshape.83
  81.9 6.8 all-to-all-done.1
  88.7 4.6 all-to-all-start.2
  93.3 8.6 scatter_custom_fusion
  101.9 7.6 reshape.81
  109.6 3.0 all-to-all-done.2
  112.5 7.3 all-to-all-start
  121.2 0.2 convert_reduce_fusion
  121.4 0.1 reshape.84
  121.5 0.1 reshape.85
  121.7 57.3 %all-to-all-done = bf16[128,2,8192]{2,1,0:T(2,128)(2,1)} async-done(((bf16[128,2,8192]{2,1,0:T(2,128)(2,1)}), bf16[128,2,8192]{2,1,0:T(2,128)(2,1)}, u32[]{:S(2)}, u32[]{:S(2)}) %all-to-all-start) | async-done | bytes 4194336 | tf_op jit(solution)/shard_map/all_to_all | solution.py:122
  179.0 7.2 reshape.82
  186.2 3.6 convolution_convert_fusion.3
  189.8 9.4 fusion.37
  199.3 0.4 fusion.14
  199.7 0.6 copy-done.8
  200.2 0.8 copy-done.2
  201.0 0.2 fusion.16
  201.2 3.7 fusion.2
  205.0 3.7 convolution_convert_fusion.1
  208.7 0.4 fusion.13
  209.1 0.8 copy-done.1
  209.9 1.6 multiply_reduce_fusion.1
  211.5 5.7 multiply_reduce_fusion
  218.6 1.7 broadcast_multiply_fusion.1
  220.3 1.8 broadcast_multiply_fusion
  222.1 2.7 copy.33
  224.9 0.1 copy.30
  225.0 134.7 %all-reduce.3.cloned.1.call-done = f32[64,1024]{1,0:T(8,128)} async-done(((f32[64,1024]{1,0:T(8,128)}), f32[64,1024]{1,0:T(8,128)}) %all-reduce.3.cloned.1.call-update) | async-done | bytes 262160
  359.7 0.8 constant_dynamic-slice_fusion
  360.5 0.1 copy.31
  360.6 0.6 multiply_add_fusion.1
  361.2 650.4 %reduce-scatter.5.cloned.1.call-done = f32[64,64]{1,0:T(8,128)} async-done(((f32[8192,64]{1,0:T(8,128)}), f32[64,64]{1,0:T(8,128)}) %reduce-scatter.5.cloned.1.call-update) | async-done | bytes 16400
  1011.6 0.8 copy.34
  1012.5 0.7 copy.32
  (158 shorter events, 2.5 us)
Async XLA Ops:
  7.2 182.7 %all-gather.4.cloned.1.call-start = ((), (), s32[]{:S(2)}) async-start(), calls=%async_computation.4 | async-start | bytes 17825792 | tf_op jit(solution)/shard_map/all_gather | solution.py:149
  71.6 17.0 %all-to-all-start.1 = ((bf16[128,1,2]{2,1,0:T(2,128)(2,1)}), bf16[128,1,2]{2,1,0:T(2,128)(2,1)S(1)}, u32[]{:S(2)}, u32[]{:S(2)}) async-start(bf16[128,1,2]{2,1,0:T(2,128)(2,1)} %all_to_all.16), calls=%async_computation.1 | async-start | bytes 131072 | tf_op jit(solution)/shard_map/all_to_all | solution.py:136
  88.7 23.9 %all-to-all-start.2 = ((bf16[128,2,1024]{2,1,0:T(2,128)(2,1)}), bf16[128,2,1024]{2,1,0:T(2,128)(2,1)S(1)}, u32[]{:S(2)}, u32[]{:S(2)}) async-start(bf16[128,2,1024]{2,1,0:T(2,128)(2,1)} %reshape.83), calls=%async_computation.2 | async-start | bytes 1048576 | tf_op jit(solution)/shard_map/all_to_all | solution.py:129
  112.5 66.4 %all-to-all-start = ((bf16[128,2,8192]{2,1,0:T(2,128)(2,1)}), bf16[128,2,8192]{2,1,0:T(2,128)(2,1)}, u32[]{:S(2)}, u32[]{:S(2)}) async-start(bf16[128,2,8192]{2,1,0:T(2,128)(2,1)} %reshape.81), calls=%async_computation | async-start | bytes 8388608 | tf_op jit(solution)/shard_map/all_to_all | solution.py:122
  119.8 239.8 %all-reduce.3.cloned.1.call-start = ((), (), s32[]{:S(2)}) async-start(), calls=%async_computation.6 | async-start | bytes 524288
  121.7 77.6 %copy-start.4 = (f32[256,1024]{1,0:T(8,128)}, f32[256,1024]{1,0:T(8,128)S(1)}, u32[]{:S(2)}) copy-start(f32[256,1024]{1,0:T(8,128)S(1)} %reshape.85) | copy-start | bytes 3145732
  121.7 64.5 %copy-start = (bf16[8192,64]{0,1:T(8,128)(2,1)S(1)}, bf16[8192,64]{0,1:T(8,128)(2,1)}, u32[]{:S(2)}) copy-start(bf16[8192,64]{0,1:T(8,128)(2,1)} %param.19) | copy-start | bytes 3145732
  189.8 9.4 copy-start.3
  199.3 1.0 copy-start.8
  200.2 0.8 copy-start.2
  205.0 3.7 copy-start.5
  205.0 3.7 copy-start.9
  209.1 0.8 copy-start.1
  220.3 791.3 %reduce-scatter.5.cloned.1.call-start = ((), (), s32[]{:S(2)}) async-start(), calls=%async_computation.5 | async-start | bytes 4227072
  222.1 2.8 copy-start.6
  222.1 138.5 %copy-start.7 = (f32[64,8]{0,1:T(8,128)S(1)}, f32[64,8]{0,1:T(8,128)}, u32[]{:S(2)}) copy-start(f32[64,8]{0,1:T(8,128)} %param.23) | copy-start | bytes 6148
Sparse Core Ops, SparseCore 0:
  10.1 152.4 all-gather.3
  220.4 139.2 all-reduce.2
  362.0 649.5 reduce-scatter.4
where the time goes:
time: 1020 us
  waiting for transfers between devices  853 us (84%)
  blocking collectives  49.3 us (5%)
  local copies, waits for them, and re-layouts  36.8 us (4%)
  matrix products  31 us (3%)
  starting transfers between devices  19.2 us (2%)
  between operations  17.4 us (2%)
    unnamed x5, waiting for transfers between devices  786 us
    all_to_all x1, waiting for transfers between devices, body(): lax.all_to_all(send_rows.reshape(devices, most_rows, width), ('grp', 'fsd...  57.3 us
    all_gather x1, blocking collectives, entering(): pieces = lax.all_gather(value, axis)  49.3 us
  transfers between devices with their start and end apart: 6, of which 5 were waited for; matrix products, arithmetic and copies ran while one was open for 5% of the time, Pallas kernels for 0%

commit v1 on v0

v1 whole, which is shorter than its diff:
```python
import jax
import jax.numpy as jnp
from jax import lax
from jax.sharding import PartitionSpec as P

STEPS = 2
BOTH = ("grp", "fsdp")
adapter_scale = 2.0
learn_rate = 0.05
epsilon = 1e-06
F32 = jnp.float32
BF16 = jnp.bfloat16


def adapter_step(rows, frozen, goal, live, cap, down, up, bound):
    cur_a, cur_b = down.astype(F32), up.astype(F32)
    for _ in range(STEPS):
        a16, b16 = cur_a.astype(BF16), cur_b.astype(BF16)
        h = jnp.dot(rows, a16, preferred_element_type=F32).astype(BF16)
        y = frozen + adapter_scale * jnp.dot(h, b16, preferred_element_type=F32)
        r = (live[:, None] * (y - goal.astype(F32)) / cap).astype(BF16)
        grad_b = adapter_scale * lax.dot_general(
            h, r, (((0,), (0,)), ((), ())), preferred_element_type=F32
        )
        back = jnp.dot(r, b16.T, preferred_element_type=F32).astype(BF16)
        grad_a = adapter_scale * lax.dot_general(
            rows, back, (((0,), (0,)), ((), ())), preferred_element_type=F32
        )
        cur_a = cur_a - learn_rate * grad_a
        cur_b = cur_b - learn_rate * grad_b
    delta_a = cur_a - down.astype(F32)
    delta_b = cur_b - up.astype(F32)
    total = jnp.sum(delta_a * delta_a) + jnp.sum(delta_b * delta_b)
    factor = jnp.minimum(1.0, bound / jnp.sqrt(total + epsilon))
    return factor * delta_a, factor * delta_b


def body(
    tokens,
    targets,
    row_owner_user,
    device_row_count,
    user_row_cap,
    value_weight,
    adapter_down,
    adapter_up,
    clip_norm_bound,
    down_noise,
    up_noise,
):
    devices = lax.axis_size(BOTH)
    myself = lax.axis_index(BOTH)
    groups = lax.axis_size("grp")
    core = lax.axis_index("grp") % 2
    per_dev, width = tokens.shape
    kv_width = targets.shape[1]
    users = user_row_cap.shape[0]
    most = 3 * per_dev // (2 * devices)
    slots = devices * most
    half = kv_width // 2

    w_half = lax.dynamic_slice(
        value_weight, (0, core * half), (value_weight.shape[0], half)
    )
    w_mine = lax.all_gather(w_half, "fsdp", axis=0, tiled=True)

    user_of = row_owner_user[:, 0]
    position = jnp.arange(per_dev, dtype=jnp.int32)
    same = (user_of[:, None] == user_of[None, :]) & (position[None, :] < position[:, None])
    rank = jnp.sum(same.astype(jnp.int32), axis=1)
    slot = user_of * most + rank
    place = (jnp.arange(slots, dtype=jnp.int32)[:, None] == slot[None, :]).astype(BF16)
    in_use = (position < device_row_count[0]).astype(BF16)
    flags = jnp.broadcast_to(in_use[:, None], (per_dev, 128))

    send = jnp.concatenate(
        [
            jnp.dot(place, tokens, preferred_element_type=F32).astype(BF16),
            jnp.dot(place, targets, preferred_element_type=F32).astype(BF16),
            jnp.dot(place, flags, preferred_element_type=F32).astype(BF16),
        ],
        axis=1,
    )
    got = lax.all_to_all(
        send.reshape(devices, most, -1), BOTH, split_axis=0, concat_axis=0, tiled=True
    ).reshape(slots, -1)
    rows = got[:, :width]
    goal = got[:, width : width + kv_width]
    used = got[:, width + kv_width].astype(F32)
    order = jnp.arange(slots, dtype=jnp.int32)
    before = (order[None, :] < order[:, None]).astype(F32)
    earlier = jnp.sum(before * used[None, :], axis=1)
    cap = jnp.sum(
        jnp.where(jnp.arange(users, dtype=jnp.int32) == myself, user_row_cap, 0)
    ).astype(F32)
    live = jnp.where((used > 0.5) & (earlier < cap), 1.0, 0.0).astype(F32)

    pairs = [(i, i ^ 1) for i in range(groups)]
    w_mine, rows = lax.optimization_barrier((w_mine, rows))
    w_other = lax.ppermute(w_mine, "grp", pairs)
    f_mine = jnp.dot(rows, w_mine, preferred_element_type=F32)
    f_other = jnp.dot(rows, w_other, preferred_element_type=F32)
    frozen = jnp.concatenate(
        [jnp.where(core == 0, f_mine, f_other), jnp.where(core == 0, f_other, f_mine)],
        axis=1,
    )
    bound = clip_norm_bound[0]
    part_a, part_b = adapter_step(
        rows, frozen, goal, live, cap, adapter_down, adapter_up, bound
    )
    a_rows, rank_dim = part_a.shape[0] // devices, part_a.shape[1]
    b_cols = part_b.shape[1] // devices
    out = jnp.concatenate(
        [
            part_a.reshape(devices, a_rows * rank_dim),
            part_b.reshape(rank_dim, devices, b_cols)
            .transpose(1, 0, 2)
            .reshape(devices, rank_dim * b_cols),
        ],
        axis=1,
    ).reshape(devices, -1, 128)
    summed = jnp.sum(
        lax.all_to_all(out, BOTH, split_axis=0, concat_axis=0, tiled=True), axis=0
    ).reshape(-1)
    cut = a_rows * rank_dim
    update_a = summed[:cut].reshape(a_rows, rank_dim) + bound * down_noise
    update_b = summed[cut:].reshape(rank_dim, b_cols) + bound * up_noise
    return update_a, update_b


def solution(mesh):
    in_specs = (
        P(BOTH, None),
        P(BOTH, None),
        P(BOTH, None),
        P(BOTH),
        P(),
        P("fsdp", None),
        P(),
        P(),
        P(),
        P(BOTH, None),
        P(None, BOTH),
    )
    out_specs = (P(BOTH, None), P(None, BOTH))
    return jax.shard_map(
        body, mesh=mesh, in_specs=in_specs, out_specs=out_specs, check_vma=False
    )
```

time: 1020 us -> 242 us (0.24)
  waiting for transfers between devices: 853 us -> 19.8 us
  blocking collectives: 49.3 us -> 113 us
  starting transfers between devices: 19.2 us -> 0.04 us
    unnamed x5 -> x1, waiting for transfers between devices: 786 us -> 0.02 us
    all_to_all x0 -> x2, blocking collectives: none -> 113 us  [the longest x1 70.5 us: body(): lax.all_to_all(send.reshape(devices, most, -1), BOTH, split_axis=0, conca...]
    all_to_all x3 -> x0, waiting for transfers between devices: 67.1 us -> none  [the longest x1 57.3 us: body(): lax.all_to_all(send_rows.reshape(devices, most_rows, width), ('grp', 'fsd...]
    all_gather x1 -> x0, blocking collectives: 49.3 us -> none  [entering(): pieces = lax.all_gather(value, axis)]
    all_gather x1, waiting for transfers between devices: 0.02 us -> 19.8 us  [body(): w_mine = lax.all_gather(w_half, 'fsdp', axis=0, tiled=True)]
    all_to_all x3 -> x0, starting transfers between devices: 19.1 us -> none  [the longest x1 7.28 us: body(): lax.all_to_all(send_rows.reshape(devices, most_rows, width), ('grp', 'fsd...]
    scatter x3 -> x0, local copies, waits for them, and re-layouts: 12.4 us -> none  [the longest x1 8.61 us: body(): jnp.zeros((slot_count, width), jnp.bfloat16).at[slot_index]]
    reshape x3 -> x8, local copies, waits for them, and re-layouts: 15.9 us -> 24 us  [the longest x1 7.7 us: body(): got = lax.all_to_all(send.reshape(devices, most, -1), BOTH, split_axis=0,...]
  transfers between devices with their start and end apart: 6 -> 2, of which waited for: 5 -> 1; matrix products, arithmetic and copies ran while one was open for 5% -> 16% of each run, Pallas kernels for 0% -> 0%
where the time goes in v1:
time: 242 us; the launch traced here: 240 us
  blocking collectives  113 us (47%)
  matrix products  38.6 us (16%)
  local copies, waits for them, and re-layouts  37.5 us (15%)
  waiting for transfers between devices  19.8 us (8%)
  between operations  17.7 us (7%)
  other arithmetic  13.6 us (6%)
    all_to_all x1, blocking collectives, body(): lax.all_to_all(send.reshape(devices, most, -1), BOTH, split_axis=0, conca...  70.5 us
    all_to_all x1, blocking collectives, body(): lax.all_to_all(out, BOTH, split_axis=0, concat_axis=0, tiled=True)  42.4 us
    all_gather x1, waiting for transfers between devices, body(): w_mine = lax.all_gather(w_half, 'fsdp', axis=0, tiled=True)  19.8 us
    dot_general x2, matrix products, adapter_step(): lax.dot_general(rows, back, (((0,), (0,)), ((), ())), preferred_element_t...  9.42 us
    reshape x1, local copies, waits for them, and re-layouts, body(): got = lax.all_to_all(send.reshape(devices, most, -1), BOTH, split_axis=0,...  7.7 us
    reshape x1, local copies, waits for them, and re-layouts, body(): send.reshape(devices, most, -1)  7.66 us
    dot_general x2, matrix products, adapter_step(): h = jnp.dot(rows, a16, preferred_element_type=F32).astype(BF16)  7.16 us
    dot_general x1, matrix products, body(): f_other = jnp.dot(rows, w_other, preferred_element_type=F32)  5.74 us
  transfers between devices with their start and end apart: 2, of which 1 were waited for; matrix products, arithmetic and copies ran while one was open for 16% of the time, Pallas kernels for 0%

profile of v1, /device:TPU:0, one launch (start us, length us, event | category | flops | bytes accessed | tf_op | source)
XLA Modules:
  0.0 240.3 jit_solution(15221596751935186003)
XLA Ops:
  7.2 0.0 copy-start
  7.2 0.0 all-gather.2.cloned.1.call-start
  7.2 2.0 constant_dynamic-slice_fusion
  9.3 0.0 all-gather.2.cloned.1.call-update
  10.0 0.9 convert_reduce_fusion
  10.9 0.7 multiply_add_fusion.2
  11.6 0.2 convolution_convert_fusion.2
  11.8 1.3 convolution_convert_fusion.1
  13.2 1.2 convolution_convert_fusion
  14.4 2.4 pad_maximum_fusion
  16.8 7.7 %reshape.63 = bf16[128,2,9344]{2,1,0:T(2,128)(2,1)} reshape(bf16[256,9344]{1,0:T(8,128)(2,1)} %pad_maximum_fusion) | data formatting | bytes 9568256 | tf_op jit(solution)/shard_map/reshape | solution.py:85
  24.4 70.5 %all_to_all.10 = bf16[128,2,9344]{2,1,0:T(2,128)(2,1)} all-to-all(bf16[128,2,9344]{2,1,0:T(2,128)(2,1)} %reshape.63), channel_id=1, replica_groups=mesh['grp'=8,'fsdp'=16] {'grp','fsdp'}, dimensions={0} | all-to-all | bytes 9568256 | tf_op jit(solution)/shard_map/all_to_all | solution.py:84
  95.0 7.7 %reshape.64 = bf16[256,9344]{1,0:T(8,128)(2,1)} reshape(bf16[128,2,9344]{2,1,0:T(2,128)(2,1)} %all_to_all.10) | data formatting | bytes 9568256 | tf_op jit(solution)/shard_map/reshape | solution.py:86
  102.7 4.7 %slice.23 = bf16[256,8192]{1,0:T(8,128)(2,1)} slice(bf16[256,9344]{1,0:T(8,128)(2,1)} %reshape.64), slice={[0:256], [0:8192]} | slice | bytes 8388608 | tf_op jit(solution)/shard_map/slice | solution.py:87
  107.4 19.8 %all-gather.2.cloned.1.call-done = bf16[8192,512]{1,0:T(8,128)(2,1)} async-done(((bf16[512,512]{1,0:T(8,128)(2,1)}), bf16[8192,512]{1,0:T(8,128)(2,1)}) %all-gather.2.cloned.1.call-update) | async-done | bytes 8388624 | tf_op jit(solution)/shard_map/all_gather | solution.py:65
  127.2 0.6 fusion.26
  129.3 1.1 convert_reduce_fusion.1
  130.4 0.1 select_reduce_fusion
  130.6 1.0 select_reduce_fusion.1
  131.6 3.6 %convolution_convert_fusion.6 = bf16[256,64]{0,1:T(8,128)(2,1)S(1)} fusion(bf16[256,8192]{1,0:T(8,128)(2,1)} %slice.23, bf16[8192,64]{0,1:T(8,128)(2,1)S(1)} %copy-done.3), kind=kOutput, calls=%fused_computation.31 | convolution fusion | flops 268451840 | bytes 5275648 | tf_op jit(solution)/shard_map/dot_general | solution.py:19
  135.2 5.7 %fusion.29 = f32[256,512]{1,0:T(8,128)S(1)} fusion(bf16[256,8192]{1,0:T(8,128)(2,1)S(1)} %copy-done.2, bf16[8192,512]{1,0:T(8,128)(2,1)} %all-gather.2.cloned.1.call-done), kind=kOutput, calls=%fused_computation.63 | convolution fusion | flops 2147483648 | bytes 13107200 | tf_op jit(solution)/shard_map/dot_general | solution.py:101
  140.9 5.7 %broadcast_select_fusion.1 = (f32[256,512]{1,0:T(8,128)S(1)}, f32[256,512]{1,0:T(8,128)S(1)}) fusion(f32[256,512]{1,0:T(8,128)S(1)} %fusion.29, pred[]{:T(512)S(6)} %eq.46, bf16[256,8192]{1,0:T(8,128)(2,1)S(1)} %copy-done.2, bf16[8192,512]{1,0:T(8,128)(2,1)} %collective-permute-done), kind=kOutput, calls=%fused_computation.40 | convolution fusion | flops 2147745792 | bytes 14155777 | tf_op jit(solution)/shard_map/dot_general | solution.py:102
  146.7 0.8 copy-done.10
  147.5 0.2 copy-done.12
  147.7 2.2 fusion.12
  149.9 3.7 %fusion.2 = f32[8192,64]{0,1:T(8,128)S(1)} fusion(bf16[256,8192]{1,0:T(8,128)(2,1)} %slice.23, bf16[8192,64]{0,1:T(8,128)(2,1)S(1)} %copy-done.3, bf16[256,1024]{1,0:T(8,128)(2,1)} %fusion.12, bf16[64,1024]{1,0:T(8,128)(2,1)S(1)} %copy-done.4), kind=kOutput, calls=%fused_computation.5 | convolution fusion | flops 303579136 | bytes 7995392 | tf_op jit(solution)/shard_map/dot_general | solution.py:26
  153.6 1.4 fusion.14
  155.0 3.6 %convolution_convert_fusion.4 = bf16[256,64]{0,1:T(8,128)(2,1)S(1)} fusion(bf16[256,8192]{1,0:T(8,128)(2,1)} %slice.23, f32[8192,64]{0,1:T(8,128)S(1)} %fusion.2), kind=kOutput, calls=%fused_computation.29 | convolution fusion | flops 268976128 | bytes 6324224 | tf_op jit(solution)/shard_map/dot_general | solution.py:19
  158.6 0.6 copy-done.5
  159.2 2.3 fusion.11
  161.5 5.7 %multiply_reduce_fusion = (f32[]{:T(128)}, f32[8192,64]{0,1:T(8,128)}) fusion(bf16[8192,64]{0,1:T(8,128)(2,1)S(1)} %copy-done.3, f32[8192,64]{0,1:T(8,128)S(1)} %fusion.2, bf16[256,8192]{1,0:T(8,128)(2,1)} %slice.23, bf16[256,1024]{1,0:T(8,128)(2,1)} %fusion.11, f32[64,1024]{1,0:T(8,128)S(1)} %fusion.14), kind=kOutput, calls=%fused_computation.8 | convolution fusion | flops 305217536 | bytes 10223620 | tf_op jit(solution)/shard_map/dot_general | solution.py:26
  167.2 1.9 multiply_reduce_fusion.1
  170.5 1.8 broadcast_multiply_fusion
  172.2 2.7 %copy.48 = f32[8192,64]{1,0:T(8,128)} copy(f32[8192,64]{0,1:T(8,128)S(1)} %broadcast_multiply_fusion) | data formatting | bytes 4194304 | tf_op jit(solution)/shard_map/mul | solution.py:35
  174.9 4.8 %reshape.65 = f32[128,4096]{1,0:T(8,128)} reshape(f32[8192,64]{1,0:T(8,128)} %copy.48) | data formatting | bytes 4194304 | tf_op jit(solution)/shard_map/reshape | solution.py:115
  179.7 0.2 copy.49
  179.9 0.2 copy.50
  180.2 0.1 copy.51
  180.3 1.8 pad_maximum_fusion.1
  182.1 2.0 copy.52
  184.1 3.5 %copy.53 = f32[128,36,128]{2,1,0:T(8,128)} copy(f32[128,36,128]{0,2,1:T(8,128)} %bitcast.33) | data formatting | bytes 4718592 | tf_op jit(solution)/shard_map/reshape | solution.py:121
  187.6 42.4 %all_to_all.11 = f32[128,36,128]{2,1,0:T(8,128)} all-to-all(f32[128,36,128]{2,1,0:T(8,128)} %copy.53), channel_id=1, replica_groups=mesh['grp'=8,'fsdp'=16] {'grp','fsdp'}, dimensions={0} | all-to-all | bytes 4718592 | tf_op jit(solution)/shard_map/all_to_all | solution.py:123
  230.0 2.0 reduce_sum.59
  232.0 0.1 reshape.69
  232.1 0.1 reshape.70
  232.2 0.1 copy.54
  232.2 0.6 multiply_add_fusion
  232.9 0.6 multiply_add_fusion.1
  (31 shorter events, 0.1 us)
Async XLA Ops:
  7.2 6.0 %copy-start = (bf16[192,8192]{1,0:T(8,128)(2,1)S(1)}, bf16[192,8192]{1,0:T(8,128)(2,1)}, u32[]{:S(2)}) copy-start(bf16[192,8192]{1,0:T(8,128)(2,1)} %param.11) | copy-start | bytes 9437188
  7.2 120.0 %all-gather.2.cloned.1.call-start = ((), (), s32[]{:S(2)}) async-start(), calls=%async_computation.2 | async-start | bytes 8912896 | tf_op jit(solution)/shard_map/all_gather | solution.py:65
  102.7 24.5 %copy-start.9 = (s32[128]{0:T(128)S(1)}, s32[128]{0:T(128)}, u32[]{:S(2)}) copy-start(s32[128]{0:T(128)} %param.15) | copy-start | bytes 1540
  102.7 28.9 %copy-start.3 = (bf16[8192,64]{0,1:T(8,128)(2,1)S(1)}, bf16[8192,64]{0,1:T(8,128)(2,1)}, u32[]{:S(2)}) copy-start(bf16[8192,64]{0,1:T(8,128)(2,1)} %param.17) | copy-start | bytes 3145732
  127.2 13.7 %collective-permute-start = (bf16[8192,512]{1,0:T(8,128)(2,1)}, bf16[8192,512]{1,0:T(8,128)(2,1)}, u32[]{:S(2)}, u32[]{:S(2)}) collective-permute-start(bf16[8192,512]{1,0:T(8,128)(2,1)} %all-gather.2.cloned.1.call-done), channel_id=1, source_target_pairs={{0,16},{16,0},{32,48},{48,32},{64,80},{80,64},{96,112},{112,96},{1... | collective-permute-start | bytes 25165832 | tf_op jit(solution)/shard_map/ppermute | solution.py:100
  128.5 6.7 %copy-start.2 = (bf16[256,8192]{1,0:T(8,128)(2,1)S(1)}, bf16[256,8192]{1,0:T(8,128)(2,1)}, u32[]{:S(2)}) copy-start(bf16[256,8192]{1,0:T(8,128)(2,1)} %slice.23) | copy-start | bytes 12582916
  135.2 11.5 %copy-start.6 = (bf16[256,64]{0,1:T(8,128)(2,1)}, bf16[256,64]{0,1:T(8,128)(2,1)S(1)}, u32[]{:S(2)}) copy-start(bf16[256,64]{0,1:T(8,128)(2,1)S(1)} %convolution_convert_fusion.6) | copy-start | bytes 98308
  140.9 6.8 %copy-start.4 = (bf16[64,1024]{1,0:T(8,128)(2,1)S(1)}, bf16[64,1024]{1,0:T(8,128)(2,1)}, u32[]{:S(2)}) copy-start(bf16[64,1024]{1,0:T(8,128)(2,1)} %param.18) | copy-start | bytes 393220
  146.7 0.8 copy-start.10
  146.7 1.0 copy-start.12
  153.6 5.6 %copy-start.11 = (f32[256,512]{1,0:T(8,128)S(1)}, f32[256,512]{1,0:T(8,128)}, u32[]{:S(2)}) copy-start(f32[256,512]{1,0:T(8,128)} %copy-done.10) | copy-start | bytes 1572868
  153.6 5.6 %copy-start.13 = (f32[256,512]{1,0:T(8,128)S(1)}, f32[256,512]{1,0:T(8,128)}, u32[]{:S(2)}) copy-start(f32[256,512]{1,0:T(8,128)} %copy-done.12) | copy-start | bytes 1572868
  158.6 0.6 copy-start.5
  184.1 49.4 %copy-start.1 = (bf16[192,8192]{1,0:T(8,128)(2,1)S(1)}, bf16[192,8192]{1,0:T(8,128)(2,1)}, u32[]{:S(2)}) copy-start(bf16[192,8192]{1,0:T(8,128)(2,1)} %param.11) | copy-start | bytes 9437188
  187.6 44.6 %copy-start.7 = (f32[64,64]{1,0:T(8,128)S(1)}, f32[64,64]{1,0:T(8,128)}, u32[]{:S(2)}) copy-start(f32[64,64]{1,0:T(8,128)} %param.20) | copy-start | bytes 49156
  187.6 45.3 %copy-start.8 = (f32[64,8]{0,1:T(8,128)S(1)}, f32[64,8]{0,1:T(8,128)}, u32[]{:S(2)}) copy-start(f32[64,8]{0,1:T(8,128)} %param.21) | copy-start | bytes 6148
Sparse Core Ops, SparseCore 0:
  10.1 117.0 all-gather.1

commit v2 on v1

v2 whole, which is shorter than its diff:
```python
import functools

import jax
import jax.numpy as jnp
from jax import lax
from jax.experimental import pallas as pl
from jax.experimental.pallas import tpu as pltpu
from jax.sharding import PartitionSpec as P

STEPS = 2
BOTH = ("grp", "fsdp")
MESH = pl.DeviceIdType.MESH
scale = 2.0
rate = 0.05
epsilon = 1e-06
F32 = jnp.float32
BF16 = jnp.bfloat16
SIDE = 4
ROWS_A = 64
SLAB = 72


def mm(a, b, ca, cb):
    return lax.dot_general(a, b, (((ca,), (cb,)), ((), ())), preferred_element_type=F32)


def slab_place(p):
    y, c, x, zh = p // 16, p // 8 % 2, p // 2 % 4, p % 2
    def code(i):
        u, v = i // 2, (i ^ (i // 2)) & 1
        return (v, u) if c == 0 else (u, v)
    return (c, *code(y), *code(x), zh)


def adapter_kernel(
    width, kv, chunk, f_ref, i_ref, got_ref, wm_ref, wo_ref, at_ref, b_ref, out_ref, mine, other, hid, a1, bcur, acc
):
    step = pl.program_id(0)
    steps = width // chunk
    slots = got_ref.shape[0]

    @pl.when(step == 0)
    def _():
        mine[...] = jnp.zeros_like(mine)
        other[...] = jnp.zeros_like(other)
        hid[...] = jnp.zeros_like(hid)

    def part(k):
        return pl.ds(pl.multiple_of(k * chunk, chunk), chunk)

    rows = got_ref[:, part(step)]
    mine[...] += mm(rows, wm_ref[...], 1, 0)
    other[...] += mm(rows, wo_ref[...], 1, 0)
    hid[...] += mm(rows, at_ref[:, part(step)], 1, 1)

    @pl.when(step == steps - 1)
    def _():
        cap, bound, core = f_ref[0], f_ref[1], i_ref[0]
        used = got_ref[:, width + kv :]
        r_i = lax.broadcasted_iota(jnp.int32, (slots, slots), 0)
        c_i = lax.broadcasted_iota(jnp.int32, (slots, slots), 1)
        before = jnp.where(c_i < r_i, 1.0, 0.0).astype(BF16)
        earlier = mm(before, used, 1, 0)
        live = jnp.where((used.astype(F32) > 0.5) & (earlier < cap), 1.0 / cap, 0.0)
        live = jnp.concatenate([live] * (kv // live.shape[1]), axis=1)
        first, second = mine[...], other[...]
        base = jnp.concatenate(
            [jnp.where(core == 0, first, second), jnp.where(core == 0, second, first)], axis=1
        ) - got_ref[:, width : width + kv].astype(F32)

        def errors(h, b16):
            y = base + scale * mm(h, b16, 1, 0)
            r = (live * y).astype(BF16)
            return r, mm(r, b16, 1, 1).astype(BF16), scale * mm(h, r, 0, 0)

        b0 = b_ref[...]
        h1 = hid[...].astype(BF16)
        _, back, grad_b = errors(h1, b0)
        bcur[...] = b0.astype(F32) - rate * grad_b
        hid[...] = jnp.zeros_like(hid)

        @pl.loop(0, steps)
        def _(k):
            x = got_ref[:, part(k)]
            a = at_ref[:, part(k)].astype(F32) - rate * (scale * mm(back, x, 0, 0))
            a1[:, part(k)] = a
            hid[...] += mm(x, a.astype(BF16), 1, 1)

        h2 = hid[...].astype(BF16)
        _, back2, grad_b2 = errors(h2, bcur[...].astype(BF16))
        delta_b = (bcur[...] - rate * grad_b2) - b0.astype(F32)
        acc[...] = jnp.zeros_like(acc)

        @pl.loop(0, steps)
        def _(k):
            x = got_ref[:, part(k)]
            d = (a1[:, part(k)] - rate * (scale * mm(back2, x, 0, 0))) - at_ref[:, part(k)].astype(F32)
            a1[:, part(k)] = d
            acc[...] += jnp.sum((d * d).reshape(d.shape[0], chunk // 128, 128), axis=1)

        total = jnp.sum(acc[...]) + jnp.sum(delta_b * delta_b)
        factor = jnp.minimum(1.0, bound / jnp.sqrt(jnp.broadcast_to(total, (8, 128)) + epsilon))
        fa = jnp.concatenate([factor] * (ROWS_A // 8), axis=0)
        pairs = width // 128
        bt = (delta_b * factor[:1, :1]).T.reshape(pairs, 16, ROWS_A)
        packed = jnp.concatenate([bt[:, :8, :], bt[:, 8:, :]], axis=2)
        for p in range(pairs):
            place = slab_place(p)
            out_ref[(*place, slice(0, ROWS_A), slice(None))] = fa * a1[:, p * 128 : (p + 1) * 128]
            out_ref[(*place, slice(ROWS_A, SLAB), slice(None))] = packed[p]


def adapter(got, w_mine, w_other, at, b, floats, ints, width, kv):
    slots, cols = got.shape
    chunk = 1024
    return pl.pallas_call(
        functools.partial(adapter_kernel, width, kv, chunk),
        grid=(width // chunk,),
        out_shape=jax.ShapeDtypeStruct((2, 2, 2, 2, 2, 2, SLAB, 128), F32),
        in_specs=[
            pl.BlockSpec(memory_space=pltpu.SMEM),
            pl.BlockSpec(memory_space=pltpu.SMEM),
            pl.BlockSpec((slots, cols), lambda k: (0, 0), pipeline_mode=pl.Buffered(1)),
            pl.BlockSpec((chunk, kv // 2), lambda k: (k, 0)),
            pl.BlockSpec((chunk, kv // 2), lambda k: (k, 0)),
            pl.BlockSpec(at.shape, lambda k: (0, 0), pipeline_mode=pl.Buffered(1)),
            pl.BlockSpec(b.shape, lambda k: (0, 0), pipeline_mode=pl.Buffered(1)),
        ],
        out_specs=pl.BlockSpec(
            (2, 2, 2, 2, 2, 2, SLAB, 128), lambda k: (0,) * 8, pipeline_mode=pl.Buffered(1)
        ),
        scratch_shapes=[
            pltpu.VMEM((slots, kv // 2), F32),
            pltpu.VMEM((slots, kv // 2), F32),
            pltpu.VMEM((slots, at.shape[0]), F32),
            pltpu.VMEM(at.shape, F32),
            pltpu.VMEM(b.shape, F32),
            pltpu.VMEM((at.shape[0], 128), F32),
        ],
        compiler_params=pltpu.CompilerParams(vmem_limit_bytes=40 << 20),
        name="adapter",
    )(floats, ints, got, w_mine, w_other, at, b)


def places():
    g, f = lax.axis_index("grp"), lax.axis_index("fsdp")
    return g // 2, g % 2, f // SIDE, f % SIDE


def low(i):
    return i + 1 - 2 * (i % 2)


def mirror(i):
    return 3 - i


def bits(i, c):
    u = i // 2
    v = (i + i // 2) % 2
    return c * u + (1 - c) * v, c * v + (1 - c) * u


def sides(i, c):
    return c * mirror(i) + (1 - c) * low(i), c * low(i) + (1 - c) * mirror(i)


CUT = 40


def reduce_kernel(
    s_ref, out_ref, a0, a1, a2, a3, a4, a5, a6, s1, b0, b1, b2, b3, b4, b5, b6, t1, send, recv
):
    y, c, x, z = places()

    def dev(y=y, c=c, x=x, z=z):
        return (y * 2 + c, x * SIDE + z)

    yb, xb, zh = bits(y, c), bits(x, c), z // 2
    yn, xn = sides(y, c), sides(x, c)
    across = dev(c=1 - c)
    over_y = [dev(y=n) for n in yn]
    over_x = [dev(x=n) for n in xn]
    over_z = [dev(z=mirror(z)), dev(z=low(z))]
    partners = [across, *over_y, *over_x, *over_z]
    barrier = pltpu.get_barrier_semaphore()
    for d in partners:
        pl.semaphore_signal(barrier, inc=1, device_id=d, device_id_type=MESH)
    pl.semaphore_wait(barrier, len(partners))

    started = []

    def go(src, dst, to):
        n = len(started)
        d = pltpu.make_async_remote_copy(
            src_ref=src, dst_ref=dst, send_sem=send.at[n], recv_sem=recv.at[n],
            device_id=to, device_id_type=MESH,
        )
        d.start()
        started.append(d)
        return d

    top, low_rows = slice(0, CUT), slice(CUT, SLAB)
    da = go(s_ref.at[1 - c, :, :, :, :, :, top], a0, across)
    db = go(s_ref.at[1 - c, :, :, :, :, :, low_rows], b0, across)

    da.wait_recv()
    s1[...] = s_ref[c, :, :, :, :, :, top] + a0[...]
    da = go(s1.at[1 - yb[0]], a1, over_y[0])
    db.wait_recv()
    t1[...] = s_ref[c, :, :, :, :, :, low_rows] + b0[...]
    db = go(t1.at[:, :, 1 - xb[0]], b1, over_x[0])

    da.wait_recv()
    a1[...] += s1[yb[0]]
    da = go(a1.at[1 - yb[1]], a2, over_y[1])
    db.wait_recv()
    b1[...] += t1[:, :, xb[0]]
    db = go(b1.at[:, :, 1 - xb[1]], b2, over_x[1])

    da.wait_recv()
    a2[...] += a1[yb[1]]
    da = go(a2.at[1 - xb[0]], a3, over_x[0])
    db.wait_recv()
    b2[...] += b1[:, :, xb[1]]
    db = go(b2.at[1 - yb[0]], b3, over_y[0])

    da.wait_recv()
    a3[...] += a2[xb[0]]
    da = go(a3.at[1 - xb[1]], a4, over_x[1])
    db.wait_recv()
    b3[...] += b2[yb[0]]
    db = go(b3.at[1 - yb[1]], b4, over_y[1])

    da.wait_recv()
    a4[...] += a3[xb[1]]
    da = go(a4.at[1 - zh], a5, over_z[0])
    db.wait_recv()
    b4[...] += b3[yb[1]]
    db = go(b4.at[1 - zh], b5, over_z[0])

    da.wait_recv()
    a5[...] += a4[zh]
    da = go(a5, a6, over_z[1])
    db.wait_recv()
    b5[...] += b4[zh]
    db = go(b5, b6, over_z[1])

    da.wait_recv()
    out_ref[top] = a5[...] + a6[...]
    db.wait_recv()
    out_ref[low_rows] = b5[...] + b6[...]
    for d in started:
        d.wait_send()


def reduce(slabs):
    def halves(n):
        two = (2, 2, 2, 2, 2)
        bufs = [pltpu.VMEM((*two[k:], n, 128), F32) for k in (0, 1, 2, 3, 4, 5)]
        return [bufs[0], *bufs[1:], pltpu.VMEM((n, 128), F32), pltpu.VMEM((*two, n, 128), F32)]

    return pl.pallas_call(
        reduce_kernel,
        out_shape=jax.ShapeDtypeStruct((SLAB, 128), F32),
        in_specs=[pl.BlockSpec(memory_space=pltpu.VMEM)],
        out_specs=pl.BlockSpec(memory_space=pltpu.VMEM),
        scratch_shapes=[
            *halves(CUT),
            *halves(SLAB - CUT),
            pltpu.SemaphoreType.DMA((14,)),
            pltpu.SemaphoreType.DMA((14,)),
        ],
        compiler_params=pltpu.CompilerParams(collective_id=0, has_side_effects=True),
        name="reduce_slabs",
    )(slabs)


def body(
    tokens,
    targets,
    row_owner_user,
    device_row_count,
    user_row_cap,
    value_weight,
    adapter_down,
    adapter_up,
    clip_norm_bound,
    down_noise,
    up_noise,
):
    devices = lax.axis_size(BOTH)
    myself = lax.axis_index(BOTH)
    groups = lax.axis_size("grp")
    core = lax.axis_index("grp") % 2
    per_dev, width = tokens.shape
    kv = targets.shape[1]
    users = user_row_cap.shape[0]
    most = 3 * per_dev // (2 * devices)
    slots = devices * most
    half = kv // 2

    w_half = lax.dynamic_slice(value_weight, (0, core * half), (value_weight.shape[0], half))
    w_mine = lax.all_gather(w_half, "fsdp", axis=0, tiled=True)

    user_of = row_owner_user[:, 0]
    position = jnp.arange(per_dev, dtype=jnp.int32)
    same = (user_of[:, None] == user_of[None, :]) & (position[None, :] < position[:, None])
    rank = jnp.sum(same.astype(jnp.int32), axis=1)
    slot = user_of * most + rank
    place = (jnp.arange(slots, dtype=jnp.int32)[:, None] == slot[None, :]).astype(BF16)
    in_use = (position < device_row_count[0]).astype(BF16)
    flags = jnp.broadcast_to(in_use[:, None], (per_dev, 128))
    cap = jnp.sum(jnp.where(jnp.arange(users, dtype=jnp.int32) == myself, user_row_cap, 0))
    bound = clip_norm_bound[0]
    floats = jnp.stack([cap.astype(F32), bound])
    ints = core.reshape(1)
    at = adapter_down.T

    send = jnp.concatenate(
        [
            jnp.dot(place, tokens, preferred_element_type=F32).astype(BF16),
            jnp.dot(place, targets, preferred_element_type=F32).astype(BF16),
            jnp.dot(place, flags, preferred_element_type=F32).astype(BF16),
        ],
        axis=1,
    )
    got = lax.all_to_all(
        send.reshape(devices, most, -1), BOTH, split_axis=0, concat_axis=0, tiled=True
    ).reshape(slots, -1)

    pairs = [(i, i ^ 1) for i in range(groups)]
    w_mine, got = lax.optimization_barrier((w_mine, got))
    w_other = lax.ppermute(w_mine, "grp", pairs)
    slabs = adapter(got, w_mine, w_other, at, adapter_up, floats, ints, width, kv)
    slab = reduce(slabs)
    odd = myself % 2
    mine = jnp.where(odd == 0, slab[:, :64], slab[:, 64:])
    update_a = mine[:ROWS_A].T + bound * down_noise
    update_b = mine[ROWS_A:].T + bound * up_noise
    return update_a, update_b


def solution(mesh):
    in_specs = (
        P(BOTH, None),
        P(BOTH, None),
        P(BOTH, None),
        P(BOTH),
        P(),
        P("fsdp", None),
        P(),
        P(),
        P(),
        P(BOTH, None),
        P(None, BOTH),
    )
    out_specs = (P(BOTH, None), P(None, BOTH))
    return jax.shard_map(
        body, mesh=mesh, in_specs=in_specs, out_specs=out_specs, check_vma=False
    )
```

time: 242 us -> 205 us (0.85)
  Pallas kernels: 0 us -> 49.2 us
  blocking collectives: 113 us -> 70.5 us
  matrix products: 38.6 us -> 2.79 us
  waiting for transfers between devices: 19.8 us -> 36 us
  local copies, waits for them, and re-layouts: 37.5 us -> 23.2 us
  other arithmetic: 13.6 us -> 6.2 us
    pallas_call x0 -> x2, Pallas kernels: none -> 49.2 us  [the longest x1 29.8 us: reduce(): pl.pallas_call(reduce_kernel, out_shape=jax.ShapeDtypeStruct((SLAB, 128),...]
    all_to_all x1 -> x0, blocking collectives: 42.4 us -> none  [body(): lax.all_to_all(out, BOTH, split_axis=0, concat_axis=0, tiled=True)]
    dot_general x10 -> x0, matrix products: 35.8 us -> none  [the longest x2 9.42 us: adapter_step(): lax.dot_general(rows, back, (((0,), (0,)), ((), ())), preferred_element_t...]
    ppermute x1, waiting for transfers between devices: 0.01 us -> 11.4 us  [body(): w_other = lax.ppermute(w_mine, 'grp', pairs)]
    reshape x6 -> x0, local copies, waits for them, and re-layouts: 8.64 us -> none  [the longest x1 4.77 us: body(): part_a.reshape(devices, a_rows * rank_dim)]
    all_gather x1, waiting for transfers between devices: 19.8 us -> 24.6 us  [body(): w_mine = lax.all_gather(w_half, 'fsdp', axis=0, tiled=True)]
    slice x3 -> x0, local copies, waits for them, and re-layouts: 4.73 us -> none  [the longest x1 4.73 us: body(): rows = got[:, :width]]
    unnamed x28 -> x18, local copies, waits for them, and re-layouts: 1.66 us -> 5.78 us
  transfers between devices with their start and end apart: 2 -> 2, of which waited for: 1 -> 2; matrix products, arithmetic and copies ran while one was open for 16% -> 11% of each run, Pallas kernels for 0% -> 0%
where the time goes in v2:
time: 205 us; the launch traced here: 204 us
  blocking collectives  70.5 us (34%)
  Pallas kernels  49.2 us (24%)
  waiting for transfers between devices  36 us (18%)
  local copies, waits for them, and re-layouts  23.2 us (11%)
  between operations  16.1 us (8%)
  other arithmetic  6.2 us (3%)
  matrix products  2.79 us (1%)
    all_to_all x1, blocking collectives, body(): lax.all_to_all(send.reshape(devices, most, -1), BOTH, split_axis=0, conca...  70.5 us
    pallas_call x1, Pallas kernels, reduce(): pl.pallas_call(reduce_kernel, out_shape=jax.ShapeDtypeStruct((SLAB, 128),...  29.8 us
    all_gather x1, waiting for transfers between devices, body(): w_mine = lax.all_gather(w_half, 'fsdp', axis=0, tiled=True)  24.6 us
    pallas_call x1, Pallas kernels, adapter(): pl.pallas_call(functools.partial(adapter_kernel, width, kv, chunk), grid=...  19.4 us
    ppermute x1, waiting for transfers between devices, body(): w_other = lax.ppermute(w_mine, 'grp', pairs)  11.4 us
    reshape x1, local copies, waits for them, and re-layouts, body(): send.reshape(devices, most, -1)  7.68 us
    reshape x1, local copies, waits for them, and re-layouts, body(): got = lax.all_to_all(send.reshape(devices, most, -1), BOTH, split_axis=0,...  7.65 us
    unnamed x18, local copies, waits for them, and re-layouts  5.78 us
  transfers between devices with their start and end apart: 2, of which 2 were waited for; matrix products, arithmetic and copies ran while one was open for 11% of the time, Pallas kernels for 0%

profile of v2, /device:TPU:0, one launch (start us, length us, event | category | flops | bytes accessed | tf_op | source)
XLA Modules:
  0.0 204.0 jit_solution(9815988413944409982)
XLA Ops:
  7.2 0.0 copy-start
  7.2 0.0 all-gather.2.cloned.1.call-start
  7.2 2.1 %constant_dynamic-slice_fusion = bf16[512,512]{1,0:T(8,128)(2,1)} fusion(bf16[512,1024]{1,0:T(8,128)(2,1)} %param.16, s32[]{:T(128)S(6)} %select_n.30), kind=kLoop, calls=%fused_computation.22 | loop fusion | bytes 1048580 | tf_op jit(solution)/shard_map/dynamic_slice | solution.py:303
  9.3 0.0 all-gather.2.cloned.1.call-update
  10.0 0.9 convert_reduce_fusion
  10.9 0.7 multiply_add_fusion
  11.6 0.2 convolution_convert_fusion.2
  11.9 1.3 convolution_convert_fusion.1
  13.2 0.0 copy-done
  13.2 1.2 convolution_convert_fusion
  14.4 2.3 %pad_maximum_fusion = bf16[256,9344]{1,0:T(8,128)(2,1)} fusion(bf16[256,128]{1,0:T(8,128)(2,1)S(1)} %convolution_convert_fusion.2, bf16[256,1024]{1,0:T(8,128)(2,1)S(1)} %convolution_convert_fusion.1, bf16[256,8192]{1,0:T(8,128)(2,1)S(1)} %convolution_convert_fusion), kind=kLoop, calls=%fused_computation.1 | loop fusion | flops 14352384 | bytes 9568256 | tf_op jit(solution)/shard_map/concatenate | solution.py:320
  16.8 7.7 %reshape.28 = bf16[128,2,9344]{2,1,0:T(2,128)(2,1)} reshape(bf16[256,9344]{1,0:T(8,128)(2,1)} %pad_maximum_fusion) | data formatting | bytes 9568256 | tf_op jit(solution)/shard_map/reshape | solution.py:329
  24.5 70.5 %all_to_all.5 = bf16[128,2,9344]{2,1,0:T(2,128)(2,1)} all-to-all(bf16[128,2,9344]{2,1,0:T(2,128)(2,1)} %reshape.28), channel_id=1, replica_groups=mesh['grp'=8,'fsdp'=16] {'grp','fsdp'}, dimensions={0} | all-to-all | bytes 9568256 | tf_op jit(solution)/shard_map/all_to_all | solution.py:328
  95.0 0.0 copy-start.7
  95.0 0.0 copy-start.5
  95.0 0.0 copy-start.4
  95.0 7.6 %reshape.29.got_ref = bf16[256,9344]{1,0:T(8,128)(2,1)} reshape(bf16[128,2,9344]{2,1,0:T(2,128)(2,1)} %all_to_all.5) | data formatting | bytes 9568256 | tf_op jit(solution)/shard_map/reshape | solution.py:330
  102.7 24.6 %all-gather.2.cloned.1.call-done.wm_ref = bf16[8192,512]{1,0:T(8,128)(2,1)} async-done(((bf16[512,512]{1,0:T(8,128)(2,1)}), bf16[8192,512]{1,0:T(8,128)(2,1)}) %all-gather.2.cloned.1.call-update) | async-done | bytes 8388624 | tf_op jit(solution)/shard_map/all_gather | solution.py:304
  127.2 0.0 collective-permute-start
  127.2 0.0 copy-done.7
  127.2 0.6 fusion.7
  129.2 0.0 copy-done.5
  129.2 0.1 copy.17
  129.3 0.1 pad_maximum_fusion.1.f_ref
  129.3 11.4 %collective-permute-done.wo_ref = bf16[8192,512]{1,0:T(8,128)(2,1)} collective-permute-done((bf16[8192,512]{1,0:T(8,128)(2,1)}, bf16[8192,512]{1,0:T(8,128)(2,1)}, u32[]{:S(2)}, u32[]{:S(2)}) %collective-permute-start) | collective-permute-done | bytes 8388640 | tf_op jit(solution)/shard_map/ppermute | solution.py:334
  140.7 0.0 copy-done.4
  140.7 0.0 copy-start.1
  140.7 2.4 %copy-done.1 = bf16[256,9344]{1,0:T(8,128)(2,1)S(1)} copy-done((bf16[256,9344]{1,0:T(8,128)(2,1)S(1)}, bf16[256,9344]{1,0:T(8,128)(2,1)}, u32[]{:S(2)}) %copy-start.1) | copy-done | bytes 4784152
  143.1 0.0 copy-start.3
  143.1 1.2 copy-done.3
  144.3 0.0 copy-start.6
  144.3 19.4 %adapter.1.s_ref = f32[2,2,2,2,2,2,72,128]{7,6,5,4,3,2,1,0:T(8,128)S(1)} custom-call(f32[2]{0:T(128)S(1)} %pad_maximum_fusion.1.f_ref, s32[1]{0:T(128)} %bitcast.1.i_ref, bf16[256,9344]{1,0:T(8,128)(2,1)S(1)} %copy-done.1, bf16[8192,512]{1,0:T(8,128)(2,1)} %all-gather.2.cloned.1.call-done.wm_ref, bf16[8192,512]{1,0:T(8,128)(2,1)} %collective-permute-done.wo_ref, ...), custom_call_target="tpu_custom_call" | custom-call | tf_op jit(solution)/shard_map/adapter/pallas_call | solution.py:116
  163.7 0.0 copy-start.2
  163.7 1.4 copy-done.2
  165.1 29.8 %reduce_slabs.1 = f32[72,128]{1,0:T(8,128)} custom-call(f32[2,2,2,2,2,2,72,128]{7,6,5,4,3,2,1,0:T(8,128)} %copy-done.2), custom_call_target="tpu_custom_call" | custom-call | tf_op jit(solution)/shard_map/reduce_slabs/pallas_call | solution.py:263
  195.0 0.9 slice_select_fusion
  195.9 0.7 copy.18
  196.6 0.0 copy-done.6
  196.6 0.6 fusion.6
  (2 shorter events, 0.0 us)
Async XLA Ops:
  7.2 6.0 %copy-start = (bf16[192,8192]{1,0:T(8,128)(2,1)S(1)}, bf16[192,8192]{1,0:T(8,128)(2,1)}, u32[]{:S(2)}) copy-start(bf16[192,8192]{1,0:T(8,128)(2,1)} %param.11) | copy-start | bytes 9437188
  7.2 120.0 %all-gather.2.cloned.1.call-start = ((), (), s32[]{:S(2)}) async-start(), calls=%async_computation.1 | async-start | bytes 8912896 | tf_op jit(solution)/shard_map/all_gather | solution.py:304
  95.0 32.2 %copy-start.7 = (s32[128]{0:T(128)S(1)}, s32[128]{0:T(128)}, u32[]{:S(2)}) copy-start(s32[128]{0:T(128)} %param.15) | copy-start | bytes 1540
  95.0 34.2 %copy-start.5 = (f32[64,64]{1,0:T(8,128)S(1)}, f32[64,64]{1,0:T(8,128)}, u32[]{:S(2)}) copy-start(f32[64,64]{1,0:T(8,128)} %param.20) | copy-start | bytes 49156
  95.0 45.7 %copy-start.4 = (bf16[64,1024]{1,0:T(8,128)(2,1)S(1)}, bf16[64,1024]{1,0:T(8,128)(2,1)}, u32[]{:S(2)}) copy-start(bf16[64,1024]{1,0:T(8,128)(2,1)} %b_ref.1) | copy-start | bytes 393220
  127.2 13.5 %collective-permute-start = (bf16[8192,512]{1,0:T(8,128)(2,1)}, bf16[8192,512]{1,0:T(8,128)(2,1)}, u32[]{:S(2)}, u32[]{:S(2)}) collective-permute-start(bf16[8192,512]{1,0:T(8,128)(2,1)} %all-gather.2.cloned.1.call-done.wm_ref), channel_id=1, source_target_pairs={{0,16},{16,0},{32,48},{48,32},{64,80},{80,64},{96,112},{112,96},{1... | collective-permute-start | bytes 25165832 | tf_op jit(solution)/shard_map/ppermute | solution.py:334
  140.7 2.4 %copy-start.1 = (bf16[256,9344]{1,0:T(8,128)(2,1)S(1)}, bf16[256,9344]{1,0:T(8,128)(2,1)}, u32[]{:S(2)}) copy-start(bf16[256,9344]{1,0:T(8,128)(2,1)} %reshape.29.got_ref) | copy-start | bytes 14352388
  143.1 1.2 copy-start.3
  144.3 52.3 %copy-start.6 = (f32[64,8]{0,1:T(8,128)S(1)}, f32[64,8]{0,1:T(8,128)}, u32[]{:S(2)}) copy-start(f32[64,8]{0,1:T(8,128)} %param.21) | copy-start | bytes 6148
  163.7 1.4 copy-start.2
Sparse Core Ops, SparseCore 0:
  10.1 117.0 all-gather.1

commit v3 on v2

v3 whole, which is shorter than its diff:
```python
import functools

import jax
import jax.numpy as jnp
from jax import lax
from jax.experimental import pallas as pl
from jax.experimental.pallas import tpu as pltpu
from jax.sharding import PartitionSpec as P

STEPS = 2
BOTH = ("grp", "fsdp")
MESH = pl.DeviceIdType.MESH
scale = 2.0
rate = 0.05
epsilon = 1e-06
F32 = jnp.float32
BF16 = jnp.bfloat16
SIDE = 4
ROWS_A = 64
SLAB = 72


def mm(a, b, ca, cb):
    return lax.dot_general(a, b, (((ca,), (cb,)), ((), ())), preferred_element_type=F32)


def slab_place(p):
    y, c, x, zh = p // 16, p // 8 % 2, p // 2 % 4, p % 2
    def code(i):
        u, v = i // 2, (i ^ (i // 2)) & 1
        return (v, u) if c == 0 else (u, v)
    return (c, *code(y), *code(x), zh)


def places():
    g, f = lax.axis_index("grp"), lax.axis_index("fsdp")
    return g // 2, g % 2, f // SIDE, f % SIDE


def low(i):
    return i + 1 - 2 * (i % 2)


def mirror(i):
    return 3 - i


def bits(i, c):
    u = i // 2
    v = (i + i // 2) % 2
    return c * u + (1 - c) * v, c * v + (1 - c) * u


def sides(i, c):
    return c * mirror(i) + (1 - c) * low(i), c * low(i) + (1 - c) * mirror(i)


ROWS_F = 16
ROWS_G = 32
AHEAD = 2
PARTS = 2
PIECE = 256
ORDER = [(1, 0), (0, 1), (3, 0), (0, 3), (1, 1), (3, 3), (1, 3), (3, 1), (2, 0), (0, 2), (2, 1), (1, 2), (2, 3), (3, 2), (2, 2)]


def flip(i, by_low, by_mirror):
    i = i + by_low * (1 - 2 * (i % 2))
    return i + by_mirror * (3 - 2 * i)


def piece(i, h, a, b):
    i0, i1, i2, i3 = i % 2, i // 2 % 2, i // 4 % 2, i // 8
    if h == 1:
        i0, i1, i2, i3 = i1, i0, i3, i2
    return flip(a, i0, i1), flip(b, i2, i3)


def main_kernel(
    f_ref, place_ref, tok_ref, tgt_ref, w_ref, at_ref, b_ref, out_ref,
    st, sx, rt, rx, pt, px, gt, gx, wf, acc, hid, a1, bcur, sq,
    fsend, frecv, gsend, grecv, wsend, wrecv, csend, crecv, local,
):
    y, c, x, z = places()
    g, f = y * 2 + c, x * SIDE + z
    a, b = (1 - c) * x + c * z, (1 - c) * z + c * x
    width = tok_ref.shape[1]
    kv = b_ref.shape[1]
    chunk = sx.shape[2]
    steps = width // chunk
    slots = place_ref.shape[0]
    half = kv // 2

    def column(pos, core):
        return pos[0] * (SIDE - 3 * core) + pos[1] * (1 + 3 * core)

    f_peers = []
    for dx, dz in ORDER:
        f_peers.append((x + dx) % SIDE * SIDE + (z + dz) % SIDE)
    g_peers = []
    for dy, dc in [(1, 0), (3, 1), (3, 0), (1, 1), (2, 0), (2, 1), (0, 1)]:
        g_peers.append((y + dy) % SIDE * 2 + (c + dc) % 2)

    barrier = pltpu.get_barrier_semaphore()
    for to in f_peers:
        pl.semaphore_signal(barrier, inc=1, device_id=(g, to), device_id_type=MESH)
    for to in g_peers:
        pl.semaphore_signal(barrier, inc=1, device_id=(to, f), device_id_type=MESH)

    keep = []
    for h in range(PARTS):
        rows = slice(h * PIECE, (h + 1) * PIECE)
        for n in range(2):
            keep.append(
                pltpu.make_async_copy(w_ref.at[rows, n * half : (n + 1) * half], wf.at[n, f, rows], local.at[2 * h + n])
            )
            keep[-1].start()

    place = place_ref[...]
    n_i = lax.broadcasted_iota(jnp.int32, (slots, slots), 0)
    o_i = lax.broadcasted_iota(jnp.int32, (slots, slots), 1)
    old = ((n_i >> 1) & 15) * 16 + (n_i >> 5) * 2 + (n_i & 1)
    turn = jnp.where(o_i == old, 1.0, 0.0).astype(BF16)

    def bufs(k):
        if k == 0:
            return st, rt, pt, gt
        return sx.at[k - 1], rx.at[k - 1], px.at[k - 1], gx.at[k - 1]

    def rows_f(i):
        return pl.ds(pl.multiple_of(i * ROWS_F, ROWS_F), ROWS_F)

    def rows_g(i):
        return pl.ds(pl.multiple_of(i * ROWS_G, ROWS_G), ROWS_G)

    def place_rows(k):
        s = bufs(k)[0]
        source = tgt_ref[...] if k == 0 else tok_ref[:, (k - 1) * chunk : k * chunk]
        s[...] = mm(place, source, 1, 0).astype(BF16)

    def start_f(k):
        s, r, _, _ = bufs(k)
        for to in f_peers:
            pltpu.make_async_remote_copy(
                src_ref=s.at[rows_f(to)], dst_ref=r.at[rows_f(f)], send_sem=fsend.at[k], recv_sem=frecv.at[k],
                device_id=(g, to), device_id_type=MESH,
            ).start()
        r[rows_f(f), :] = s[rows_f(f), :]

    def turn_rows(k):
        _, r, p, q = bufs(k)
        most = r.at[: slots - ROWS_F]
        pltpu.make_async_copy(most, most, frecv.at[k]).wait()
        p[...] = mm(turn, r[...], 1, 0).astype(BF16)
        for to in g_peers:
            pltpu.make_async_remote_copy(
                src_ref=p.at[rows_g(to)], dst_ref=q.at[rows_g(g)], send_sem=gsend.at[k], recv_sem=grecv.at[k],
                device_id=(to, f), device_id_type=MESH,
            ).start()
        q[rows_g(g), :] = p[rows_g(g), :]

    def end_g(k):
        q = bufs(k)[3]
        most = q.at[: slots - ROWS_G]
        pltpu.make_async_copy(most, most, grecv.at[k]).wait()

    def weight(i, h):
        return wf.at[c, column(piece(i, h, a, b), c), h * PIECE : (h + 1) * PIECE]

    def pass_on(i, h):
        level = i.bit_length()
        to_ref = weight(i, h)
        if i == 0:
            src = w_ref.at[h * PIECE : (h + 1) * PIECE, pl.ds(pl.multiple_of(c * half, half), half)]
        else:
            src = to_ref
            pltpu.make_async_copy(src, src, wrecv.at[h, i]).wait()
            swap(i, h)
        for n in range(level, 4):
            to = column(piece(1 << n, h, a, b), c)
            pltpu.make_async_remote_copy(
                src_ref=src, dst_ref=to_ref, send_sem=wsend.at[h], recv_sem=wrecv.at[h, (1 << n) + i],
                device_id=(g, to), device_id_type=MESH,
            ).start()

    def swap(i, h):
        ref = weight(i, h)
        pltpu.make_async_remote_copy(
            src_ref=ref, dst_ref=ref, send_sem=csend.at[h], recv_sem=crecv.at[h, i],
            device_id=(y * 2 + 1 - c, f), device_id_type=MESH,
        ).start()

    def other_column(i, h):
        return column(piece(i, h, b, a), 1 - c)

    def add(n, col, h):
        per = chunk // (PARTS * PIECE)
        x_cols = gx[col // per, :, pl.ds(pl.multiple_of(col % per * (PARTS * PIECE) + h * PIECE, PIECE), PIECE)]
        acc[n] += mm(x_cols, wf[n, col, h * PIECE : (h + 1) * PIECE, :], 1, 0)

    place_rows(0)
    pl.semaphore_wait(barrier, len(f_peers) + len(g_peers))
    for h in range(PARTS):
        pass_on(0, h)
    start_f(0)
    acc[...] = jnp.zeros_like(acc)
    hid[...] = jnp.zeros_like(hid)
    todo = {3: [1], 5: [2, 3], 7: [4, 5, 6, 7]}
    for k in range(1, steps + 1 + AHEAD):
        if k <= steps:
            place_rows(k)
            start_f(k)
        if k >= AHEAD:
            turn_rows(k - AHEAD)
        for i in todo.get(k, []):
            for h in range(PARTS):
                pass_on(i, h)

    end_g(0)
    for k in range(1, steps + 1):
        end_g(k)
        hid[...] += mm(gx[k - 1], at_ref[:, (k - 1) * chunk : k * chunk], 1, 1)
    for d in keep:
        d.wait()
    for n in range(2):
        for h in range(PARTS):
            add(n, f, h)

    @pl.loop(1, 8)
    def _(i):
        for h in range(PARTS):
            add(c, column(piece(i, h, a, b), c), h)
            col = other_column(i, h)
            ref = wf.at[1 - c, col, h * PIECE : (h + 1) * PIECE]
            pltpu.make_async_copy(ref, ref, crecv.at[h, i]).wait()
            add(1 - c, col, h)

    @pl.loop(8, 16)
    def _(i):
        for h in range(PARTS):
            ref = weight(i, h)
            pltpu.make_async_copy(ref, ref, wrecv.at[h, i]).wait()
            swap(i, h)
            add(c, column(piece(i, h, a, b), c), h)

    @pl.loop(8, 16)
    def _(i):
        for h in range(PARTS):
            col = other_column(i, h)
            ref = wf.at[1 - c, col, h * PIECE : (h + 1) * PIECE]
            pltpu.make_async_copy(ref, ref, crecv.at[h, i]).wait()
            add(1 - c, col, h)

    cap, bound = f_ref[0], f_ref[1]
    used = gt[:, kv:]
    before = jnp.where(o_i < n_i, 1.0, 0.0).astype(BF16)
    earlier = mm(before, used, 1, 0)
    live = jnp.where((used.astype(F32) > 0.5) & (earlier < cap), 1.0 / cap, 0.0)
    live = jnp.concatenate([live] * (kv // live.shape[1]), axis=1)
    base = jnp.concatenate([acc[0], acc[1]], axis=1) - gt[:, :kv].astype(F32)

    def part(k):
        return pl.ds(pl.multiple_of(k * chunk, chunk), chunk)

    def errors(h, b16):
        r = (live * (base + scale * mm(h, b16, 1, 0))).astype(BF16)
        return mm(r, b16, 1, 1).astype(BF16), scale * mm(h, r, 0, 0)

    b0 = b_ref[...]
    back, grad_b = errors(hid[...].astype(BF16), b0)
    bcur[...] = b0.astype(F32) - rate * grad_b
    hid[...] = jnp.zeros_like(hid)

    @pl.loop(0, steps)
    def _(k):
        rows = gx[k]
        now = at_ref[:, part(k)].astype(F32) - rate * (scale * mm(back, rows, 0, 0))
        a1[:, part(k)] = now
        hid[...] += mm(rows, now.astype(BF16), 1, 1)

    back2, grad_b2 = errors(hid[...].astype(BF16), bcur[...].astype(BF16))
    delta_b = (bcur[...] - rate * grad_b2) - b0.astype(F32)
    sq[...] = jnp.zeros_like(sq)

    @pl.loop(0, steps)
    def _(k):
        d = (a1[:, part(k)] - rate * (scale * mm(back2, gx[k], 0, 0))) - at_ref[:, part(k)].astype(F32)
        a1[:, part(k)] = d
        sq[...] += jnp.sum((d * d).reshape(d.shape[0], chunk // 128, 128), axis=1)

    total = jnp.sum(sq[...]) + jnp.sum(delta_b * delta_b)
    factor = jnp.minimum(1.0, bound / jnp.sqrt(jnp.broadcast_to(total, (8, 128)) + epsilon))
    fa = jnp.concatenate([factor] * (ROWS_A // 8), axis=0)
    pairs = width // 128
    bt = (delta_b * factor[:1, :1]).T.reshape(pairs, 16, ROWS_A)
    packed = jnp.concatenate([bt[:, :8, :], bt[:, 8:, :]], axis=2)
    for p in range(pairs):
        spot = slab_place(p)
        out_ref[(*spot, slice(0, ROWS_A), slice(None))] = fa * a1[:, p * 128 : (p + 1) * 128]
        out_ref[(*spot, slice(ROWS_A, SLAB), slice(None))] = packed[p]

    for k in range(steps + 1):
        s, _, p, _ = bufs(k)
        most = s.at[: slots - ROWS_F]
        pltpu.make_async_copy(most, most, fsend.at[k]).wait()
        most = p.at[: slots - ROWS_G]
        pltpu.make_async_copy(most, most, gsend.at[k]).wait()
    for h in range(PARTS):
        sent = wf.at[0, :15, h * PIECE : (h + 1) * PIECE]
        pltpu.make_async_copy(sent, sent, wsend.at[h]).wait()
        pltpu.make_async_copy(sent, sent, csend.at[h]).wait()


def main(floats, place, tokens, goals, weight, at, b):
    slots, width, kv = place.shape[0], tokens.shape[1], b.shape[1]
    chunk = 1024
    steps = width // chunk
    extra = goals.shape[1]
    whole = pl.BlockSpec(memory_space=pltpu.VMEM)
    four = [pltpu.VMEM((slots, extra), BF16), pltpu.VMEM((steps, slots, chunk), BF16)] * 4
    dma = pltpu.SemaphoreType.DMA
    return pl.pallas_call(
        main_kernel,
        out_shape=jax.ShapeDtypeStruct((2, 2, 2, 2, 2, 2, SLAB, 128), F32),
        in_specs=[
            pl.BlockSpec(memory_space=pltpu.SMEM),
            whole,
            whole,
            whole,
            pl.BlockSpec(memory_space=pl.ANY),
            whole,
            whole,
        ],
        out_specs=whole,
        scratch_shapes=[
            *four,
            pltpu.VMEM((2, SIDE * SIDE, *[weight.shape[0], kv // 2]), BF16),
            pltpu.VMEM((2, slots, kv // 2), F32),
            pltpu.VMEM((slots, at.shape[0]), F32),
            pltpu.VMEM(at.shape, F32),
            pltpu.VMEM(b.shape, F32),
            pltpu.VMEM((at.shape[0], 128), F32),
            dma((steps + 1,)),
            dma((steps + 1,)),
            dma((steps + 1,)),
            dma((steps + 1,)),
            dma((PARTS,)),
            dma((PARTS, 16)),
            dma((PARTS,)),
            dma((PARTS, 16)),
            dma((2 * PARTS,)),
        ],
        compiler_params=pltpu.CompilerParams(
            collective_id=1, has_side_effects=True, vmem_limit_bytes=60 << 20
        ),
        name="exchange_and_adapt",
    )(floats, place, tokens, goals, weight, at, b)


CUT = 40


def reduce_kernel(
    s_ref, out_ref, a0, a1, a2, a3, a4, a5, a6, s1, b0, b1, b2, b3, b4, b5, b6, t1, send, recv
):
    y, c, x, z = places()

    def dev(y=y, c=c, x=x, z=z):
        return (y * 2 + c, x * SIDE + z)

    yb, xb, zh = bits(y, c), bits(x, c), z // 2
    yn, xn = sides(y, c), sides(x, c)
    across = dev(c=1 - c)
    over_y = [dev(y=n) for n in yn]
    over_x = [dev(x=n) for n in xn]
    over_z = [dev(z=mirror(z)), dev(z=low(z))]
    partners = [across, *over_y, *over_x, *over_z]
    barrier = pltpu.get_barrier_semaphore()
    for d in partners:
        pl.semaphore_signal(barrier, inc=1, device_id=d, device_id_type=MESH)
    pl.semaphore_wait(barrier, len(partners))

    started = []

    def go(src, dst, to):
        n = len(started)
        d = pltpu.make_async_remote_copy(
            src_ref=src, dst_ref=dst, send_sem=send.at[n], recv_sem=recv.at[n],
            device_id=to, device_id_type=MESH,
        )
        d.start()
        started.append(d)
        return d

    top, low_rows = slice(0, CUT), slice(CUT, SLAB)
    da = go(s_ref.at[1 - c, :, :, :, :, :, top], a0, across)
    db = go(s_ref.at[1 - c, :, :, :, :, :, low_rows], b0, across)

    da.wait_recv()
    s1[...] = s_ref[c, :, :, :, :, :, top] + a0[...]
    da = go(s1.at[1 - yb[0]], a1, over_y[0])
    db.wait_recv()
    t1[...] = s_ref[c, :, :, :, :, :, low_rows] + b0[...]
    db = go(t1.at[:, :, 1 - xb[0]], b1, over_x[0])

    da.wait_recv()
    a1[...] += s1[yb[0]]
    da = go(a1.at[1 - yb[1]], a2, over_y[1])
    db.wait_recv()
    b1[...] += t1[:, :, xb[0]]
    db = go(b1.at[:, :, 1 - xb[1]], b2, over_x[1])

    da.wait_recv()
    a2[...] += a1[yb[1]]
    da = go(a2.at[1 - xb[0]], a3, over_x[0])
    db.wait_recv()
    b2[...] += b1[:, :, xb[1]]
    db = go(b2.at[1 - yb[0]], b3, over_y[0])

    da.wait_recv()
    a3[...] += a2[xb[0]]
    da = go(a3.at[1 - xb[1]], a4, over_x[1])
    db.wait_recv()
    b3[...] += b2[yb[0]]
    db = go(b3.at[1 - yb[1]], b4, over_y[1])

    da.wait_recv()
    a4[...] += a3[xb[1]]
    da = go(a4.at[1 - zh], a5, over_z[0])
    db.wait_recv()
    b4[...] += b3[yb[1]]
    db = go(b4.at[1 - zh], b5, over_z[0])

    da.wait_recv()
    a5[...] += a4[zh]
    da = go(a5, a6, over_z[1])
    db.wait_recv()
    b5[...] += b4[zh]
    db = go(b5, b6, over_z[1])

    da.wait_recv()
    out_ref[top] = a5[...] + a6[...]
    db.wait_recv()
    out_ref[low_rows] = b5[...] + b6[...]
    for d in started:
        d.wait_send()


def reduce(slabs):
    def halves(n):
        two = (2, 2, 2, 2, 2)
        bufs = [pltpu.VMEM((*two[k:], n, 128), F32) for k in (0, 1, 2, 3, 4, 5)]
        return [bufs[0], *bufs[1:], pltpu.VMEM((n, 128), F32), pltpu.VMEM((*two, n, 128), F32)]

    return pl.pallas_call(
        reduce_kernel,
        out_shape=jax.ShapeDtypeStruct((SLAB, 128), F32),
        in_specs=[pl.BlockSpec(memory_space=pltpu.VMEM)],
        out_specs=pl.BlockSpec(memory_space=pltpu.VMEM),
        scratch_shapes=[
            *halves(CUT),
            *halves(SLAB - CUT),
            pltpu.SemaphoreType.DMA((14,)),
            pltpu.SemaphoreType.DMA((14,)),
        ],
        compiler_params=pltpu.CompilerParams(collective_id=0, has_side_effects=True),
        name="reduce_slabs",
    )(slabs)


def body(
    tokens,
    targets,
    row_owner_user,
    device_row_count,
    user_row_cap,
    value_weight,
    adapter_down,
    adapter_up,
    clip_norm_bound,
    down_noise,
    up_noise,
):
    devices = lax.axis_size(BOTH)
    myself = lax.axis_index(BOTH)
    across = lax.axis_size("fsdp")
    per_dev = tokens.shape[0]
    users = user_row_cap.shape[0]
    most = 3 * per_dev // (2 * devices)
    slots = devices * most

    user_of = row_owner_user[:, 0]
    position = jnp.arange(per_dev, dtype=jnp.int32)
    same = (user_of[:, None] == user_of[None, :]) & (position[None, :] < position[:, None])
    rank = jnp.sum(same.astype(jnp.int32), axis=1)
    slot = (user_of % across) * ROWS_F + user_of // across * most + rank
    place = (jnp.arange(slots, dtype=jnp.int32)[:, None] == slot[None, :]).astype(BF16)
    in_use = (position < device_row_count[0]).astype(BF16)
    goals = jnp.concatenate([targets, jnp.broadcast_to(in_use[:, None], (per_dev, 128))], axis=1)
    cap = jnp.sum(jnp.where(jnp.arange(users, dtype=jnp.int32) == myself, user_row_cap, 0))
    bound = clip_norm_bound[0]
    floats = jnp.stack([cap.astype(F32), bound])
    slabs = main(floats, place, tokens, goals, value_weight, adapter_down.T, adapter_up)
    slab = reduce(slabs)
    odd = myself % 2
    mine = jnp.where(odd == 0, slab[:, :64], slab[:, 64:])
    update_a = mine[:ROWS_A].T + bound * down_noise
    update_b = mine[ROWS_A:].T + bound * up_noise
    return update_a, update_b


def solution(mesh):
    in_specs = (
        P(BOTH, None),
        P(BOTH, None),
        P(BOTH, None),
        P(BOTH),
        P(),
        P("fsdp", None),
        P(),
        P(),
        P(),
        P(BOTH, None),
        P(None, BOTH),
    )
    out_specs = (P(BOTH, None), P(None, BOTH))
    return jax.shard_map(
        body, mesh=mesh, in_specs=in_specs, out_specs=out_specs, check_vma=False
    )
```

time: 205 us -> 178 us (0.87)
  Pallas kernels: 49.2 us -> 166 us
  blocking collectives: 70.5 us -> 0 us
  waiting for transfers between devices: 36 us -> 0 us
  local copies, waits for them, and re-layouts: 23.2 us -> 0.87 us
  between operations: 16.1 us -> 2.65 us
  matrix products: 2.79 us -> 0 us
    pallas_call x1, Pallas kernels: 19.4 us -> 136 us  [main(): pl.pallas_call(main_kernel, out_shape=jax.ShapeDtypeStruct((2, 2, 2, 2, 2...]
    all_to_all x1 -> x0, blocking collectives: 70.5 us -> none  [body(): lax.all_to_all(send.reshape(devices, most, -1), BOTH, split_axis=0, conca...]
    all_gather x1 -> x0, waiting for transfers between devices: 24.6 us -> none  [body(): w_mine = lax.all_gather(w_half, 'fsdp', axis=0, tiled=True)]
    reshape x2 -> x0, local copies, waits for them, and re-layouts: 15.3 us -> none  [the longest x1 7.68 us: body(): send.reshape(devices, most, -1)]
    ppermute x1 -> x0, waiting for transfers between devices: 11.4 us -> none  [body(): w_other = lax.ppermute(w_mine, 'grp', pairs)]
    unnamed x18 -> x6, local copies, waits for them, and re-layouts: 5.78 us -> 0.78 us
    dot_general x3 -> x0, matrix products: 2.79 us -> none  [the longest x1 1.29 us: body(): jnp.dot(place, targets, preferred_element_type=F32).astype(BF16)]
    dynamic_slice x1 -> x0, local copies, waits for them, and re-layouts: 2.07 us -> none  [body(): lax.dynamic_slice(value_weight, (0, core * half), (value_weight.shape[0],...]
  transfers between devices with their start and end apart: 2 -> 0, of which waited for: 2 -> 0; matrix products, arithmetic and copies ran while one was open for 11% -> 0% of each run, Pallas kernels for 0% -> 0%
where the time goes in v3:
time: 178 us; the launch traced here: 177 us
  Pallas kernels  166 us (93%)
  other arithmetic  7.52 us (4%)
  between operations  2.65 us (1%)
    pallas_call x1, Pallas kernels, main(): pl.pallas_call(main_kernel, out_shape=jax.ShapeDtypeStruct((2, 2, 2, 2, 2...  136 us
    pallas_call x1, Pallas kernels, reduce(): pl.pallas_call(reduce_kernel, out_shape=jax.ShapeDtypeStruct((SLAB, 128),...  30 us

profile of v3, /device:TPU:0, one launch (start us, length us, event | category | flops | bytes accessed | tf_op | source)
XLA Modules:
  0.0 177.1 jit_solution(187496825910430216)
XLA Ops:
  0.6 1.3 fusion.7
  3.2 0.6 pad_maximum_fusion.1.f_ref
  3.8 0.9 convert_reduce_fusion
  4.8 0.7 fusion.6
  5.5 0.7 fusion.place_ref
  6.8 0.1 broadcast_in_dim.6
  6.9 1.8 %pad_maximum_fusion.tgt_ref = bf16[192,1152]{1,0:T(8,128)(2,1)} fusion(bf16[192,128]{1,0:T(8,128)(2,1)S(1)} %broadcast_in_dim.6, bf16[192,1024]{1,0:T(8,128)(2,1)} %param.12), kind=kLoop, calls=%fused_computation | loop fusion | flops 884736 | bytes 884736 | tf_op jit(solution)/shard_map/concatenate | solution.py:498
  8.7 0.0 copy-start
  8.7 0.0 copy-start.1
  8.7 136.1 %exchange_and_adapt.1.s_ref = f32[2,2,2,2,2,2,72,128]{7,6,5,4,3,2,1,0:T(8,128)} custom-call(f32[2]{0:T(128)} %pad_maximum_fusion.1.f_ref, bf16[256,192]{1,0:T(8,128)(2,1)} %fusion.place_ref, bf16[192,8192]{1,0:T(8,128)(2,1)} %tok_ref.1, bf16[192,1152]{1,0:T(8,128)(2,1)} %pad_maximum_fusion.tgt_ref, bf16[512,1024]{1,0:T(8,128)(2,1)} %w_ref.1, ...), custom_call_target="tpu_custom_call" | custom-call | tf_op jit(solution)/shard_map/exchange_and_adapt/pallas_call | solution.py:321
  144.8 30.0 %reduce_slabs.1 = f32[72,128]{1,0:T(8,128)} custom-call(f32[2,2,2,2,2,2,72,128]{7,6,5,4,3,2,1,0:T(8,128)} %exchange_and_adapt.1.s_ref), custom_call_target="tpu_custom_call" | custom-call | tf_op jit(solution)/shard_map/reduce_slabs/pallas_call | solution.py:454
  174.8 0.9 slice_select_fusion
  175.7 0.0 copy-done
  175.7 0.1 copy.15
  175.8 0.7 copy.16
  176.5 0.0 copy-done.1
  176.5 0.6 fusion.3
  (2 shorter events, 0.0 us)
Async XLA Ops:
  8.7 167.0 %copy-start = (f32[64,64]{1,0:T(8,128)S(1)}, f32[64,64]{1,0:T(8,128)}, u32[]{:S(2)}) copy-start(f32[64,64]{1,0:T(8,128)} %param.20) | copy-start | bytes 49156
  8.7 167.8 %copy-start.1 = (f32[64,8]{0,1:T(8,128)S(1)}, f32[64,8]{0,1:T(8,128)}, u32[]{:S(2)}) copy-start(f32[64,8]{0,1:T(8,128)} %param.21) | copy-start | bytes 6148

commit v4 on v2

v4 whole, which is shorter than its diff:
```python
import functools

import jax
import jax.numpy as jnp
from jax import lax
from jax.experimental import pallas as pl
from jax.experimental.pallas import tpu as pltpu
from jax.sharding import PartitionSpec as P

STEPS = 2
BOTH = ("grp", "fsdp")
MESH = pl.DeviceIdType.MESH
scale = 2.0
rate = 0.05
epsilon = 1e-06
F32 = jnp.float32
BF16 = jnp.bfloat16
SIDE = 4
ROWS_A = 64
SLAB = 72


def mm(a, b, ca, cb):
    return lax.dot_general(a, b, (((ca,), (cb,)), ((), ())), preferred_element_type=F32)


def slab_place(p):
    y, c, x, zh = p // 16, p // 8 % 2, p // 2 % 4, p % 2
    def code(i):
        u, v = i // 2, (i ^ (i // 2)) & 1
        return (v, u) if c == 0 else (u, v)
    return (c, *code(y), *code(x), zh)


def places():
    g, f = lax.axis_index("grp"), lax.axis_index("fsdp")
    return g // 2, g % 2, f // SIDE, f % SIDE


def low(i):
    return i + 1 - 2 * (i % 2)


def mirror(i):
    return 3 - i


def bits(i, c):
    u = i // 2
    v = (i + i // 2) % 2
    return c * u + (1 - c) * v, c * v + (1 - c) * u


def sides(i, c):
    return c * mirror(i) + (1 - c) * low(i), c * low(i) + (1 - c) * mirror(i)


CUT = 40


def sum_slabs(s_ref, out_ref, a0, a1, a2, a3, a4, a5, a6, s1, b0, b1, b2, b3, b4, b5, b6, t1, send, recv):
    y, c, x, z = places()

    def dev(y=y, c=c, x=x, z=z):
        return (y * 2 + c, x * SIDE + z)

    yb, xb, zh = bits(y, c), bits(x, c), z // 2
    yn, xn = sides(y, c), sides(x, c)
    across = dev(c=1 - c)
    over_y = [dev(y=n) for n in yn]
    over_x = [dev(x=n) for n in xn]
    over_z = [dev(z=mirror(z)), dev(z=low(z))]
    started = []

    def go(src, dst, to):
        n = len(started)
        d = pltpu.make_async_remote_copy(
            src_ref=src, dst_ref=dst, send_sem=send.at[n], recv_sem=recv.at[n],
            device_id=to, device_id_type=MESH,
        )
        d.start()
        started.append(d)
        return d

    top, low_rows = slice(0, CUT), slice(CUT, SLAB)
    da = go(s_ref.at[1 - c, :, :, :, :, :, top], a0, across)
    db = go(s_ref.at[1 - c, :, :, :, :, :, low_rows], b0, across)

    da.wait_recv()
    s1[...] = s_ref[c, :, :, :, :, :, top] + a0[...]
    da = go(s1.at[1 - yb[0]], a1, over_y[0])
    db.wait_recv()
    t1[...] = s_ref[c, :, :, :, :, :, low_rows] + b0[...]
    db = go(t1.at[:, :, 1 - xb[0]], b1, over_x[0])

    da.wait_recv()
    a1[...] += s1[yb[0]]
    da = go(a1.at[1 - yb[1]], a2, over_y[1])
    db.wait_recv()
    b1[...] += t1[:, :, xb[0]]
    db = go(b1.at[:, :, 1 - xb[1]], b2, over_x[1])

    da.wait_recv()
    a2[...] += a1[yb[1]]
    da = go(a2.at[1 - xb[0]], a3, over_x[0])
    db.wait_recv()
    b2[...] += b1[:, :, xb[1]]
    db = go(b2.at[1 - yb[0]], b3, over_y[0])

    da.wait_recv()
    a3[...] += a2[xb[0]]
    da = go(a3.at[1 - xb[1]], a4, over_x[1])
    db.wait_recv()
    b3[...] += b2[yb[0]]
    db = go(b3.at[1 - yb[1]], b4, over_y[1])

    da.wait_recv()
    a4[...] += a3[xb[1]]
    da = go(a4.at[1 - zh], a5, over_z[0])
    db.wait_recv()
    b4[...] += b3[yb[1]]
    db = go(b4.at[1 - zh], b5, over_z[0])

    da.wait_recv()
    a5[...] += a4[zh]
    da = go(a5, a6, over_z[1])
    db.wait_recv()
    b5[...] += b4[zh]
    db = go(b5, b6, over_z[1])

    da.wait_recv()
    out_ref[top] = a5[...] + a6[...]
    db.wait_recv()
    out_ref[low_rows] = b5[...] + b6[...]
    for d in started:
        d.wait_send()


ROWS_F = 16
ROWS_G = 32
AHEAD = 2
PARTS = 2
PIECE = 256
ORDER = [(1, 0), (0, 1), (3, 0), (0, 3), (1, 1), (3, 3), (1, 3), (3, 1), (2, 0), (0, 2), (2, 1), (1, 2), (2, 3), (3, 2), (2, 2)]


def flip(i, by_low, by_mirror):
    i = i + by_low * (1 - 2 * (i % 2))
    return i + by_mirror * (3 - 2 * i)


def piece(i, h, a, b):
    i0, i1, i2, i3 = i % 2, i // 2 % 2, i // 4 % 2, i // 8
    if h == 1:
        i0, i1, i2, i3 = i1, i0, i3, i2
    return flip(a, i0, i1), flip(b, i2, i3)


def main_kernel(
    cap_ref, count_ref, bound_ref, user_ref, tok_ref, tgt_ref, w_ref, down_ref, b_ref, out_ref,
    place_ref, at_ref, st, sx, rt, rx, pt, px, gt, gx, wf, acc, hid, a1, bcur, sq, slabs,
    a_bufs, b_bufs, fsend, frecv, gsend, grecv, wsend, wrecv, csend, crecv, local, ssend, srecv,
):
    y, c, x, z = places()
    g, f = y * 2 + c, x * SIDE + z
    a, b = (1 - c) * x + c * z, (1 - c) * z + c * x
    width = tok_ref.shape[1]
    kv = b_ref.shape[1]
    chunk = sx.shape[2]
    steps = width // chunk
    slots = st.shape[0]
    half = kv // 2

    def column(pos, core):
        return pos[0] * (SIDE - 3 * core) + pos[1] * (1 + 3 * core)

    f_peers = []
    for dx, dz in ORDER:
        f_peers.append((x + dx) % SIDE * SIDE + (z + dz) % SIDE)
    g_peers = []
    for dy, dc in [(1, 0), (3, 1), (3, 0), (1, 1), (2, 0), (2, 1), (0, 1)]:
        g_peers.append((y + dy) % SIDE * 2 + (c + dc) % 2)

    barrier = pltpu.get_barrier_semaphore()
    for to in f_peers:
        pl.semaphore_signal(barrier, inc=1, device_id=(g, to), device_id_type=MESH)
    for to in g_peers:
        pl.semaphore_signal(barrier, inc=1, device_id=(to, f), device_id_type=MESH)

    keep = []
    for h in range(PARTS):
        rows = slice(h * PIECE, (h + 1) * PIECE)
        for n in range(2):
            keep.append(
                pltpu.make_async_copy(w_ref.at[rows, n * half : (n + 1) * half], wf.at[n, f, rows], local.at[2 * h + n])
            )
            keep[-1].start()

    user = user_ref[...]
    per = user.shape[0]
    u_i = lax.broadcasted_iota(jnp.int32, (per, per), 0)
    v_i = lax.broadcasted_iota(jnp.int32, (per, per), 1)
    lane = lax.broadcasted_iota(jnp.int32, (per, 128), 1)
    named = jnp.where(lane == user, 1.0, 0.0)
    below = jnp.where(v_i < u_i, 1.0, 0.0).astype(BF16)
    rank = jnp.sum(mm(below, named.astype(BF16), 1, 0) * named, axis=1, keepdims=True).astype(jnp.int32)
    slot = (user & 15) * ROWS_F + (user >> 4) * 2 + rank
    s_i = lax.broadcasted_iota(jnp.int32, (per, slots), 1)
    place_ref[...] = jnp.where(s_i == slot, 1.0, 0.0).T.astype(BF16)
    count = count_ref[0]
    flags = jnp.where(lax.broadcasted_iota(jnp.int32, (per, 128), 0) < count, 1.0, 0.0).astype(BF16)
    place = place_ref[...]
    n_i = lax.broadcasted_iota(jnp.int32, (slots, slots), 0)
    o_i = lax.broadcasted_iota(jnp.int32, (slots, slots), 1)
    old = ((n_i >> 1) & 15) * 16 + (n_i >> 5) * 2 + (n_i & 1)
    turn = jnp.where(o_i == old, 1.0, 0.0).astype(BF16)

    def bufs(k):
        if k == 0:
            return st, rt, pt, gt
        return sx.at[k - 1], rx.at[k - 1], px.at[k - 1], gx.at[k - 1]

    def rows_f(i):
        return pl.ds(pl.multiple_of(i * ROWS_F, ROWS_F), ROWS_F)

    def rows_g(i):
        return pl.ds(pl.multiple_of(i * ROWS_G, ROWS_G), ROWS_G)

    def place_rows(k):
        s = bufs(k)[0]
        if k == 0:
            s[:, :kv] = mm(place, tgt_ref[...], 1, 0).astype(BF16)
            s[:, kv:] = mm(place, flags, 1, 0).astype(BF16)
        else:
            s[...] = mm(place, tok_ref[:, (k - 1) * chunk : k * chunk], 1, 0).astype(BF16)

    def start_f(k):
        s, r, _, _ = bufs(k)
        for to in f_peers:
            pltpu.make_async_remote_copy(
                src_ref=s.at[rows_f(to)], dst_ref=r.at[rows_f(f)], send_sem=fsend.at[k], recv_sem=frecv.at[k],
                device_id=(g, to), device_id_type=MESH,
            ).start()
        r[rows_f(f), :] = s[rows_f(f), :]

    def turn_rows(k):
        _, r, p, q = bufs(k)
        most = r.at[: slots - ROWS_F]
        pltpu.make_async_copy(most, most, frecv.at[k]).wait()
        p[...] = mm(turn, r[...], 1, 0).astype(BF16)
        for to in g_peers:
            pltpu.make_async_remote_copy(
                src_ref=p.at[rows_g(to)], dst_ref=q.at[rows_g(g)], send_sem=gsend.at[k], recv_sem=grecv.at[k],
                device_id=(to, f), device_id_type=MESH,
            ).start()
        q[rows_g(g), :] = p[rows_g(g), :]

    def end_g(k):
        q = bufs(k)[3]
        most = q.at[: slots - ROWS_G]
        pltpu.make_async_copy(most, most, grecv.at[k]).wait()

    def weight(i, h):
        return wf.at[c, column(piece(i, h, a, b), c), h * PIECE : (h + 1) * PIECE]

    def pass_on(i, h):
        level = i.bit_length()
        to_ref = weight(i, h)
        if i == 0:
            src = w_ref.at[h * PIECE : (h + 1) * PIECE, pl.ds(pl.multiple_of(c * half, half), half)]
        else:
            src = to_ref
            pltpu.make_async_copy(src, src, wrecv.at[h, i]).wait()
            swap(i, h)
        for n in range(level, 4):
            to = column(piece(1 << n, h, a, b), c)
            pltpu.make_async_remote_copy(
                src_ref=src, dst_ref=to_ref, send_sem=wsend.at[h], recv_sem=wrecv.at[h, (1 << n) + i],
                device_id=(g, to), device_id_type=MESH,
            ).start()

    def swap(i, h):
        ref = weight(i, h)
        pltpu.make_async_remote_copy(
            src_ref=ref, dst_ref=ref, send_sem=csend.at[h], recv_sem=crecv.at[h, i],
            device_id=(y * 2 + 1 - c, f), device_id_type=MESH,
        ).start()

    def other_column(i, h):
        return column(piece(i, h, b, a), 1 - c)

    def add(n, col, h):
        per = chunk // (PARTS * PIECE)
        x_cols = gx[col // per, :, pl.ds(pl.multiple_of(col % per * (PARTS * PIECE) + h * PIECE, PIECE), PIECE)]
        acc[n] += mm(x_cols, wf[n, col, h * PIECE : (h + 1) * PIECE, :], 1, 0)

    place_rows(0)
    pl.semaphore_wait(barrier, len(f_peers) + len(g_peers))
    start_f(0)
    place_rows(1)
    start_f(1)
    acc[...] = jnp.zeros_like(acc)
    hid[...] = jnp.zeros_like(hid)
    for k in range(steps):
        cols = slice(k * chunk, (k + 1) * chunk)
        at_ref[:, cols] = down_ref[cols, :].astype(F32).T.astype(BF16)
    todo = {1: [0], 6: [1], 8: [2, 3], 10: [4, 5, 6, 7]}
    for k in range(1, steps + 1 + AHEAD):
        if 1 < k <= steps:
            place_rows(k)
            start_f(k)
        if k >= AHEAD:
            turn_rows(k - AHEAD)
        for i in todo.get(k, []):
            for h in range(PARTS):
                pass_on(i, h)

    end_g(0)
    for k in range(1, steps + 1):
        end_g(k)
        hid[...] += mm(gx[k - 1], at_ref[:, (k - 1) * chunk : k * chunk], 1, 1)
    for d in keep:
        d.wait()
    for n in range(2):
        for h in range(PARTS):
            add(n, f, h)

    @pl.loop(1, 8)
    def _(i):
        for h in range(PARTS):
            add(c, column(piece(i, h, a, b), c), h)
            col = other_column(i, h)
            ref = wf.at[1 - c, col, h * PIECE : (h + 1) * PIECE]
            pltpu.make_async_copy(ref, ref, crecv.at[h, i]).wait()
            add(1 - c, col, h)

    @pl.loop(8, 16)
    def _(i):
        for h in range(PARTS):
            ref = weight(i, h)
            pltpu.make_async_copy(ref, ref, wrecv.at[h, i]).wait()
            swap(i, h)
            add(c, column(piece(i, h, a, b), c), h)

    @pl.loop(8, 16)
    def _(i):
        for h in range(PARTS):
            col = other_column(i, h)
            ref = wf.at[1 - c, col, h * PIECE : (h + 1) * PIECE]
            pltpu.make_async_copy(ref, ref, crecv.at[h, i]).wait()
            add(1 - c, col, h)

    cap, bound = cap_ref[g * SIDE * SIDE + f].astype(F32), bound_ref[0]
    used = gt[:, kv:]
    before = jnp.where(o_i < n_i, 1.0, 0.0).astype(BF16)
    earlier = mm(before, used, 1, 0)
    live = jnp.where((used.astype(F32) > 0.5) & (earlier < cap), 1.0 / cap, 0.0)
    live = jnp.concatenate([live] * (kv // live.shape[1]), axis=1)
    base = jnp.concatenate([acc[0], acc[1]], axis=1) - gt[:, :kv].astype(F32)

    def part(k):
        return pl.ds(pl.multiple_of(k * chunk, chunk), chunk)

    def errors(h, b16):
        r = (live * (base + scale * mm(h, b16, 1, 0))).astype(BF16)
        return mm(r, b16, 1, 1).astype(BF16), scale * mm(h, r, 0, 0)

    b0 = b_ref[...]
    back, grad_b = errors(hid[...].astype(BF16), b0)
    bcur[...] = b0.astype(F32) - rate * grad_b
    hid[...] = jnp.zeros_like(hid)

    @pl.loop(0, steps)
    def _(k):
        rows = gx[k]
        now = at_ref[:, part(k)].astype(F32) - rate * (scale * mm(back, rows, 0, 0))
        a1[:, part(k)] = now
        hid[...] += mm(rows, now.astype(BF16), 1, 1)

    back2, grad_b2 = errors(hid[...].astype(BF16), bcur[...].astype(BF16))
    delta_b = (bcur[...] - rate * grad_b2) - b0.astype(F32)
    sq[...] = jnp.zeros_like(sq)

    @pl.loop(0, steps)
    def _(k):
        d = (a1[:, part(k)] - rate * (scale * mm(back2, gx[k], 0, 0))) - at_ref[:, part(k)].astype(F32)
        a1[:, part(k)] = d
        sq[...] += jnp.sum((d * d).reshape(d.shape[0], chunk // 128, 128), axis=1)

    total = jnp.sum(sq[...]) + jnp.sum(delta_b * delta_b)
    factor = jnp.minimum(1.0, bound / jnp.sqrt(jnp.broadcast_to(total, (8, 128)) + epsilon))
    fa = jnp.concatenate([factor] * (ROWS_A // 8), axis=0)
    pairs = width // 128
    bt = (delta_b * factor[:1, :1]).T.reshape(pairs, 16, ROWS_A)
    packed = jnp.concatenate([bt[:, :8, :], bt[:, 8:, :]], axis=2)
    for p in range(pairs):
        spot = slab_place(p)
        slabs[(*spot, slice(0, ROWS_A), slice(None))] = fa * a1[:, p * 128 : (p + 1) * 128]
        slabs[(*spot, slice(ROWS_A, SLAB), slice(None))] = packed[p]
    sum_slabs(slabs, out_ref, *a_bufs, *b_bufs, ssend, srecv)

    for k in range(steps + 1):
        s, _, p, _ = bufs(k)
        most = s.at[: slots - ROWS_F]
        pltpu.make_async_copy(most, most, fsend.at[k]).wait()
        most = p.at[: slots - ROWS_G]
        pltpu.make_async_copy(most, most, gsend.at[k]).wait()
    for h in range(PARTS):
        sent = wf.at[0, :15, h * PIECE : (h + 1) * PIECE]
        pltpu.make_async_copy(sent, sent, wsend.at[h]).wait()
        pltpu.make_async_copy(sent, sent, csend.at[h]).wait()


def main(caps, count, bound, user, tokens, goals, weight, down, b):
    width, kv = tokens.shape[1], b.shape[1]
    slots = ROWS_F * SIDE * SIDE
    chunk = 1024
    steps = width // chunk
    extra = kv + 128
    whole = pl.BlockSpec(memory_space=pltpu.VMEM)
    scalars = pl.BlockSpec(memory_space=pltpu.SMEM)
    four = [pltpu.VMEM((slots, extra), BF16), pltpu.VMEM((steps, slots, chunk), BF16)] * 4
    dma = pltpu.SemaphoreType.DMA

    def halves(n):
        two = (2, 2, 2, 2, 2)
        bufs = [pltpu.VMEM((*two[k:], n, 128), F32) for k in range(6)]
        return (*bufs, pltpu.VMEM((n, 128), F32), pltpu.VMEM((*two, n, 128), F32))

    return pl.pallas_call(
        main_kernel,
        out_shape=jax.ShapeDtypeStruct((SLAB, 128), F32),
        in_specs=[scalars] * 3 + [whole] * 3 + [pl.BlockSpec(memory_space=pl.ANY)] + [whole] * 2,
        out_specs=whole,
        scratch_shapes=[
            pltpu.VMEM((slots, tokens.shape[0]), BF16),
            pltpu.VMEM((down.shape[1], width), BF16),
            *four,
            pltpu.VMEM((2, SIDE * SIDE, weight.shape[0], kv // 2), BF16),
            pltpu.VMEM((2, slots, kv // 2), F32),
            pltpu.VMEM((slots, down.shape[1]), F32),
            pltpu.VMEM((down.shape[1], width), F32),
            pltpu.VMEM(b.shape, F32),
            pltpu.VMEM((down.shape[1], 128), F32),
            pltpu.VMEM((2, 2, 2, 2, 2, 2, SLAB, 128), F32),
            halves(CUT),
            halves(SLAB - CUT),
            dma((steps + 1,)),
            dma((steps + 1,)),
            dma((steps + 1,)),
            dma((steps + 1,)),
            dma((PARTS,)),
            dma((PARTS, 16)),
            dma((PARTS,)),
            dma((PARTS, 16)),
            dma((2 * PARTS,)),
            dma((14,)),
            dma((14,)),
        ],
        compiler_params=pltpu.CompilerParams(
            collective_id=0, has_side_effects=True, vmem_limit_bytes=62 << 20
        ),
        name="exchange_and_adapt",
    )(caps, count, bound, user, tokens, goals, weight, down, b)


def body(
    tokens,
    targets,
    row_owner_user,
    device_row_count,
    user_row_cap,
    value_weight,
    adapter_down,
    adapter_up,
    clip_norm_bound,
    down_noise,
    up_noise,
):
    myself = lax.axis_index(BOTH)
    bound = clip_norm_bound[0]
    slab = main(
        user_row_cap, device_row_count, clip_norm_bound, row_owner_user, tokens, targets, value_weight,
        adapter_down, adapter_up,
    )
    odd = myself % 2
    mine = jnp.where(odd == 0, slab[:, :64], slab[:, 64:])
    update_a = mine[:ROWS_A].T + bound * down_noise
    update_b = mine[ROWS_A:].T + bound * up_noise
    return update_a, update_b


def solution(mesh):
    in_specs = (
        P(BOTH, None),
        P(BOTH, None),
        P(BOTH, None),
        P(BOTH),
        P(),
        P("fsdp", None),
        P(),
        P(),
        P(),
        P(BOTH, None),
        P(None, BOTH),
    )
    out_specs = (P(BOTH, None), P(None, BOTH))
    return jax.shard_map(
        body, mesh=mesh, in_specs=in_specs, out_specs=out_specs, check_vma=False
    )
```

time: 205 us -> 154 us (0.75)
  Pallas kernels: 49.2 us -> 145 us
  blocking collectives: 70.5 us -> 0 us
  waiting for transfers between devices: 36 us -> 0 us
  local copies, waits for them, and re-layouts: 23.2 us -> 4.99 us
  between operations: 16.1 us -> 1.96 us
  other arithmetic: 6.2 us -> 1.53 us
  matrix products: 2.79 us -> 0 us
    pallas_call x2 -> x1, Pallas kernels: 49.2 us -> 145 us  [main(): pl.pallas_call(main_kernel, out_shape=jax.ShapeDtypeStruct((SLAB, 128), F...]
    all_to_all x1 -> x0, blocking collectives: 70.5 us -> none  [body(): lax.all_to_all(send.reshape(devices, most, -1), BOTH, split_axis=0, conca...]
    all_gather x1 -> x0, waiting for transfers between devices: 24.6 us -> none  [body(): w_mine = lax.all_gather(w_half, 'fsdp', axis=0, tiled=True)]
    reshape x2 -> x0, local copies, waits for them, and re-layouts: 15.3 us -> none  [the longest x1 7.68 us: body(): send.reshape(devices, most, -1)]
    ppermute x1 -> x0, waiting for transfers between devices: 11.4 us -> none  [body(): w_other = lax.ppermute(w_mine, 'grp', pairs)]
    dot_general x3 -> x0, matrix products: 2.79 us -> none  [the longest x1 1.29 us: body(): jnp.dot(place, targets, preferred_element_type=F32).astype(BF16)]
    concatenate x1 -> x0, other arithmetic: 2.34 us -> none  [body(): jnp.concatenate([jnp.dot(place, tokens, preferred_element_type=F32).astyp...]
    dynamic_slice x1 -> x0, local copies, waits for them, and re-layouts: 2.07 us -> none  [body(): lax.dynamic_slice(value_weight, (0, core * half), (value_weight.shape[0],...]
  transfers between devices with their start and end apart: 2 -> 0, of which waited for: 2 -> 0; matrix products, arithmetic and copies ran while one was open for 11% -> 0% of each run, Pallas kernels for 0% -> 0%
where the time goes in v4:
time: 154 us; the launch traced here: 153 us
  Pallas kernels  145 us (94%)
  local copies, waits for them, and re-layouts  4.99 us (3%)
  between operations  1.96 us (1%)
    pallas_call x1, Pallas kernels, main(): pl.pallas_call(main_kernel, out_shape=jax.ShapeDtypeStruct((SLAB, 128), F...  145 us
    unnamed x8, local copies, waits for them, and re-layouts  4.99 us

profile of v4, /device:TPU:0, one launch (start us, length us, event | category | flops | bytes accessed | tf_op | source)
XLA Modules:
  0.0 153.2 jit_solution(15647882326923241570)
XLA Ops:
  1.9 1.4 copy.13.user_ref
  3.4 2.8 %copy.14.down_ref = bf16[8192,64]{1,0:T(8,128)(2,1)} copy(bf16[8192,64]{0,1:T(8,128)(2,1)} %param.17) | data formatting | bytes 2097152 | tf_op args[6]
  6.1 0.0 copy-start
  6.1 0.0 copy-start.1
  6.1 144.7 %exchange_and_adapt.1 = f32[72,128]{1,0:T(8,128)} custom-call(s32[128]{0:T(128)} %cap_ref.1, s32[1]{0:T(128)S(6)} %copy.17.count_ref, f32[1]{0:T(128)} %copy.18.bound_ref, s32[192,1]{1,0:T(8,128)} %copy.13.user_ref, bf16[192,8192]{1,0:T(8,128)(2,1)} %tok_ref.1, bf16[192,1024]{1,0:T(8,128)(2,1)} %tgt_ref.1, bf16[512,1024]{1,0:T(8,128)(2,1)} %w_ref.1, ...), custom_call_target="tpu_custom_call" | custom-call | tf_op jit(solution)/shard_map/exchange_and_adapt/pallas_call | solution.py:430
  150.9 0.9 slice_select_fusion
  151.8 0.0 copy-done
  151.8 0.1 copy.15
  151.9 0.7 copy.16
  152.6 0.0 copy-done.1
  152.6 0.6 fusion.1
  (1 shorter events, 0.0 us)
Async XLA Ops:
  6.1 145.7 %copy-start = (f32[64,64]{1,0:T(8,128)S(1)}, f32[64,64]{1,0:T(8,128)}, u32[]{:S(2)}) copy-start(f32[64,64]{1,0:T(8,128)} %param.20) | copy-start | bytes 49156
  6.1 146.5 %copy-start.1 = (f32[64,8]{0,1:T(8,128)S(1)}, f32[64,8]{0,1:T(8,128)}, u32[]{:S(2)}) copy-start(f32[64,8]{0,1:T(8,128)} %param.21) | copy-start | bytes 6148

commit v5 on v4

--- a/solution.py
+++ b/solution.py
@@ -24,14 +24,6 @@
     return lax.dot_general(a, b, (((ca,), (cb,)), ((), ())), preferred_element_type=F32)
 
 
-def slab_place(p):
-    y, c, x, zh = p // 16, p // 8 % 2, p // 2 % 4, p % 2
-    def code(i):
-        u, v = i // 2, (i ^ (i // 2)) & 1
-        return (v, u) if c == 0 else (u, v)
-    return (c, *code(y), *code(x), zh)
-
-
 def places():
     g, f = lax.axis_index("grp"), lax.axis_index("fsdp")
     return g // 2, g % 2, f // SIDE, f % SIDE
@@ -55,85 +47,97 @@
     return c * mirror(i) + (1 - c) * low(i), c * low(i) + (1 - c) * mirror(i)
 
 
-CUT = 40
-
-
-def sum_slabs(s_ref, out_ref, a0, a1, a2, a3, a4, a5, a6, s1, b0, b1, b2, b3, b4, b5, b6, t1, send, recv):
+ROUTES = [
+    ("y1", "y2", "x1", "x2", "ring"),
+    ("x1", "x2", "y1", "y2", "ring"),
+    ("z", "y1", "y2", "x1", "x2", "pair"),
+]
+THIRD = SLAB // len(ROUTES)
+FIRST_SEM = SIDE + 1
+SUM_SEMS = FIRST_SEM + sum(len(r) + 2 * ("ring" in r) for r in ROUTES)
+
+
+def sum_slabs(kept, taken, factor, far, chains, send, recv):
     y, c, x, z = places()
 
     def dev(y=y, c=c, x=x, z=z):
         return (y * 2 + c, x * SIDE + z)
 
-    yb, xb, zh = bits(y, c), bits(x, c), z // 2
-    yn, xn = sides(y, c), sides(x, c)
-    across = dev(c=1 - c)
-    over_y = [dev(y=n) for n in yn]
-    over_x = [dev(x=n) for n in xn]
-    over_z = [dev(z=mirror(z)), dev(z=low(z))]
+    yb, xb, yn, xn = bits(y, c), bits(x, c), sides(y, c), sides(x, c)
+    bit = {"y1": yb[0], "y2": yb[1], "x1": xb[0], "x2": xb[1], "z": z // 2}
+    to = {
+        "y1": dev(y=yn[0]),
+        "y2": dev(y=yn[1]),
+        "x1": dev(x=xn[0]),
+        "x2": dev(x=xn[1]),
+        "z": dev(z=mirror(z)),
+        "pair": dev(z=low(z)),
+    }
     started = []
 
-    def go(src, dst, to):
-        n = len(started)
+    def go(src, dst, device):
+        n = FIRST_SEM + len(started)
         d = pltpu.make_async_remote_copy(
             src_ref=src, dst_ref=dst, send_sem=send.at[n], recv_sem=recv.at[n],
-            device_id=to, device_id_type=MESH,
+            device_id=device, device_id_type=MESH,
         )
         d.start()
         started.append(d)
         return d
 
-    top, low_rows = slice(0, CUT), slice(CUT, SLAB)
-    da = go(s_ref.at[1 - c, :, :, :, :, :, top], a0, across)
-    db = go(s_ref.at[1 - c, :, :, :, :, :, low_rows], b0, across)
-
-    da.wait_recv()
-    s1[...] = s_ref[c, :, :, :, :, :, top] + a0[...]
-    da = go(s1.at[1 - yb[0]], a1, over_y[0])
-    db.wait_recv()
-    t1[...] = s_ref[c, :, :, :, :, :, low_rows] + b0[...]
-    db = go(t1.at[:, :, 1 - xb[0]], b1, over_x[0])
-
-    da.wait_recv()
-    a1[...] += s1[yb[0]]
-    da = go(a1.at[1 - yb[1]], a2, over_y[1])
-    db.wait_recv()
-    b1[...] += t1[:, :, xb[0]]
-    db = go(b1.at[:, :, 1 - xb[1]], b2, over_x[1])
-
-    da.wait_recv()
-    a2[...] += a1[yb[1]]
-    da = go(a2.at[1 - xb[0]], a3, over_x[0])
-    db.wait_recv()
-    b2[...] += b1[:, :, xb[1]]
-    db = go(b2.at[1 - yb[0]], b3, over_y[0])
-
-    da.wait_recv()
-    a3[...] += a2[xb[0]]
-    da = go(a3.at[1 - xb[1]], a4, over_x[1])
-    db.wait_recv()
-    b3[...] += b2[yb[0]]
-    db = go(b3.at[1 - yb[1]], b4, over_y[1])
-
-    da.wait_recv()
-    a4[...] += a3[xb[1]]
-    da = go(a4.at[1 - zh], a5, over_z[0])
-    db.wait_recv()
-    b4[...] += b3[yb[1]]
-    db = go(b4.at[1 - zh], b5, over_z[0])
-
-    da.wait_recv()
-    a5[...] += a4[zh]
-    da = go(a5, a6, over_z[1])
-    db.wait_recv()
-    b5[...] += b4[zh]
-    db = go(b5, b6, over_z[1])
-
-    da.wait_recv()
-    out_ref[top] = a5[...] + a6[...]
-    db.wait_recv()
-    out_ref[low_rows] = b5[...] + b6[...]
+    near = jnp.concatenate([factor] * (THIRD // 8), axis=0)
+    away = jnp.concatenate([far] * (THIRD // 8), axis=0)
+    now, dims, flying = [], [], []
+
+    def at(ref, left, dim, i):
+        return ref.at[(slice(None),) * left.index(dim) + (i,)]
+
+    def launch(n, step):
+        route, bufs = ROUTES[n], chains[n]
+        dim, ref, left = route[step], now[n], dims[n]
+        into = bufs[step + 1]
+        if dim == "ring":
+            flying[n] = [
+                go(ref.at[(z + j) % SIDE // 2], into.at[j - 1], dev(z=(z + j) % SIDE)) for j in range(1, SIDE)
+            ]
+        elif dim == "pair":
+            flying[n] = [go(ref, into, to[dim])]
+        else:
+            flying[n] = [go(at(ref, left, dim, 1 - bit[dim]), into, to[dim])]
+
+    def land(n, step):
+        route, bufs = ROUTES[n], chains[n]
+        dim, ref, left = route[step], now[n], dims[n]
+        into = bufs[step + 1]
+        for d in flying[n]:
+            d.wait_recv()
+        if dim == "ring":
+            return ref[z // 2] + into[0] + into[1] + into[2]
+        if dim == "pair":
+            return ref[...] + into[...]
+        into[...] += at(ref, left, dim, bit[dim])[...]
+        now[n] = into
+        dims[n] = [v for v in left if v != dim]
+        return None
+
+    results = [None] * len(ROUTES)
+    for n in range(len(ROUTES)):
+        rows = slice(n * THIRD, (n + 1) * THIRD)
+        ref = chains[n][0]
+        ref[...] = near * kept[:, :, :, :, :, rows] + away * taken[:, :, :, :, :, rows]
+        now.append(ref)
+        dims.append(["y1", "y2", "x1", "x2", "z"])
+        flying.append(None)
+        launch(n, 0)
+    for step in range(max(len(r) for r in ROUTES)):
+        for n, route in enumerate(ROUTES):
+            if step < len(route):
+                results[n] = land(n, step)
+                if step + 1 < len(route):
+                    launch(n, step + 1)
     for d in started:
         d.wait_send()
+    return jnp.concatenate(results, axis=0)
 
 
 ROWS_F = 16
@@ -157,9 +161,9 @@
 
 
 def main_kernel(
-    cap_ref, count_ref, bound_ref, user_ref, tok_ref, tgt_ref, w_ref, down_ref, b_ref, out_ref,
-    place_ref, at_ref, st, sx, rt, rx, pt, px, gt, gx, wf, acc, hid, a1, bcur, sq, slabs,
-    a_bufs, b_bufs, fsend, frecv, gsend, grecv, wsend, wrecv, csend, crecv, local, ssend, srecv,
+    cap_ref, count_ref, bound_ref, user_ref, tok_ref, tgt_ref, w_ref, at_ref, b_ref, na_ref, nb_ref,
+    oa_ref, ob_ref, place_ref, st, sx, rt, rx, pt, px, gt, gx, wf, acc, hid, a1, bcur, sq,
+    given, kept, taken, packed, own_factor, far_factor, chains, fsend, frecv, gsend, grecv, wsend, wrecv, csend, crecv, local, ssend, srecv,
 ):
     y, c, x, z = places()
     g, f = y * 2 + c, x * SIDE + z
@@ -197,16 +201,14 @@
             keep[-1].start()
 
     user = user_ref[...]
-    per = user.shape[0]
+    per = user.shape[1]
     u_i = lax.broadcasted_iota(jnp.int32, (per, per), 0)
     v_i = lax.broadcasted_iota(jnp.int32, (per, per), 1)
-    lane = lax.broadcasted_iota(jnp.int32, (per, 128), 1)
-    named = jnp.where(lane == user, 1.0, 0.0)
-    below = jnp.where(v_i < u_i, 1.0, 0.0).astype(BF16)
-    rank = jnp.sum(mm(below, named.astype(BF16), 1, 0) * named, axis=1, keepdims=True).astype(jnp.int32)
+    named = jnp.where(lax.broadcasted_iota(jnp.int32, (128, per), 0) == user, 1.0, 0.0)
+    above = jnp.where(u_i < v_i, 1.0, 0.0).astype(BF16)
+    rank = jnp.sum(mm(named.astype(BF16), above, 1, 0) * named, axis=0, keepdims=True).astype(jnp.int32)
     slot = (user & 15) * ROWS_F + (user >> 4) * 2 + rank
-    s_i = lax.broadcasted_iota(jnp.int32, (per, slots), 1)
-    place_ref[...] = jnp.where(s_i == slot, 1.0, 0.0).T.astype(BF16)
+    place_ref[...] = jnp.where(lax.broadcasted_iota(jnp.int32, (slots, per), 0) == slot, 1.0, 0.0).astype(BF16)
     count = count_ref[0]
     flags = jnp.where(lax.broadcasted_iota(jnp.int32, (per, 128), 0) < count, 1.0, 0.0).astype(BF16)
     place = place_ref[...]
@@ -301,9 +303,6 @@
     start_f(1)
     acc[...] = jnp.zeros_like(acc)
     hid[...] = jnp.zeros_like(hid)
-    for k in range(steps):
-        cols = slice(k * chunk, (k + 1) * chunk)
-        at_ref[:, cols] = down_ref[cols, :].astype(F32).T.astype(BF16)
     todo = {1: [0], 6: [1], 8: [2, 3], 10: [4, 5, 6, 7]}
     for k in range(1, steps + 1 + AHEAD):
         if 1 < k <= steps:
@@ -381,23 +380,45 @@
     delta_b = (bcur[...] - rate * grad_b2) - b0.astype(F32)
     sq[...] = jnp.zeros_like(sq)
 
-    @pl.loop(0, steps)
-    def _(k):
-        d = (a1[:, part(k)] - rate * (scale * mm(back2, gx[k], 0, 0))) - at_ref[:, part(k)].astype(F32)
-        a1[:, part(k)] = d
-        sq[...] += jnp.sum((d * d).reshape(d.shape[0], chunk // 128, 128), axis=1)
+    bt = delta_b.T.reshape(width // 128, 16, ROWS_A)
+    packed[...] = jnp.concatenate([bt[:, :8, :], bt[:, 8:, :]], axis=2)
+    other_core = (y * 2 + 1 - c, f)
+
+    def to_core(src, dst, n):
+        return pltpu.make_async_remote_copy(
+            src_ref=src, dst_ref=dst, send_sem=ssend.at[n], recv_sem=srecv.at[n],
+            device_id=other_core, device_id_type=MESH,
+        )
+
+    first = []
+    for to_far in (True, False):
+        core = 1 - c if to_far else c
+        slabs = given if to_far else kept
+        for yy in range(SIDE):
+            k = yy * 2 + core
+            d = (a1[:, part(k)] - rate * (scale * mm(back2, gx[k], 0, 0))) - at_ref[:, part(k)].astype(F32)
+            sq[...] += jnp.sum((d * d).reshape(d.shape[0], chunk // 128, 128), axis=1)
+            y1, y2 = bits(yy, core)
+            for p in range(chunk // 128):
+                x1, x2 = bits(p // 2, core)
+                slabs[y1, y2, x1, x2, p % 2, :ROWS_A, :] = d[:, p * 128 : (p + 1) * 128]
+                slabs[y1, y2, x1, x2, p % 2, ROWS_A:, :] = packed[k * (chunk // 128) + p]
+            if to_far:
+                first.append(to_core(given.at[y1, y2], taken.at[y1, y2], yy))
+                first[-1].start()
 
     total = jnp.sum(sq[...]) + jnp.sum(delta_b * delta_b)
-    factor = jnp.minimum(1.0, bound / jnp.sqrt(jnp.broadcast_to(total, (8, 128)) + epsilon))
-    fa = jnp.concatenate([factor] * (ROWS_A // 8), axis=0)
-    pairs = width // 128
-    bt = (delta_b * factor[:1, :1]).T.reshape(pairs, 16, ROWS_A)
-    packed = jnp.concatenate([bt[:, :8, :], bt[:, 8:, :]], axis=2)
-    for p in range(pairs):
-        spot = slab_place(p)
-        slabs[(*spot, slice(0, ROWS_A), slice(None))] = fa * a1[:, p * 128 : (p + 1) * 128]
-        slabs[(*spot, slice(ROWS_A, SLAB), slice(None))] = packed[p]
-    sum_slabs(slabs, out_ref, *a_bufs, *b_bufs, ssend, srecv)
+    own_factor[...] = jnp.minimum(1.0, bound / jnp.sqrt(jnp.broadcast_to(total, (8, 128)) + epsilon))
+    first.append(to_core(own_factor, far_factor, SIDE))
+    first[-1].start()
+    for d in first:
+        d.wait_recv()
+    slab = sum_slabs(kept, taken, own_factor[...], far_factor[...], chains, ssend, srecv)
+    val = jnp.where(z % 2 == 1, slab[:, ROWS_A:], slab[:, :ROWS_A])
+    oa_ref[...] = val[:ROWS_A].T + bound * na_ref[...]
+    ob_ref[...] = val[ROWS_A:] + bound * nb_ref[...]
+    for d in first:
+        d.wait_send()
 
     for k in range(steps + 1):
         s, _, p, _ = bufs(k)
@@ -411,7 +432,7 @@
         pltpu.make_async_copy(sent, sent, csend.at[h]).wait()
 
 
-def main(caps, count, bound, user, tokens, goals, weight, down, b):
+def main(caps, count, bound, user, tokens, goals, weight, at, b, noise_a, noise_b):
     width, kv = tokens.shape[1], b.shape[1]
     slots = ROWS_F * SIDE * SIDE
     chunk = 1024
@@ -422,29 +443,38 @@
     four = [pltpu.VMEM((slots, extra), BF16), pltpu.VMEM((steps, slots, chunk), BF16)] * 4
     dma = pltpu.SemaphoreType.DMA
 
-    def halves(n):
-        two = (2, 2, 2, 2, 2)
-        bufs = [pltpu.VMEM((*two[k:], n, 128), F32) for k in range(6)]
-        return (*bufs, pltpu.VMEM((n, 128), F32), pltpu.VMEM((*two, n, 128), F32))
+    slabs = pltpu.VMEM((2, 2, 2, 2, 2, SLAB, 128), F32)
+
+    def chain(route):
+        left, bufs = 5, []
+        for dim in ("start", *route):
+            if dim in ("y1", "y2", "x1", "x2", "z"):
+                left -= 1
+            lead = (SIDE - 1,) if dim == "ring" else (2,) * left
+            bufs.append(pltpu.VMEM((*lead, THIRD, 128), F32))
+        return tuple(bufs)
 
     return pl.pallas_call(
         main_kernel,
-        out_shape=jax.ShapeDtypeStruct((SLAB, 128), F32),
-        in_specs=[scalars] * 3 + [whole] * 3 + [pl.BlockSpec(memory_space=pl.ANY)] + [whole] * 2,
-        out_specs=whole,
+        out_shape=tuple(jax.ShapeDtypeStruct(n.shape, F32) for n in (noise_a, noise_b)),
+        in_specs=[scalars] * 3 + [whole] * 3 + [pl.BlockSpec(memory_space=pl.ANY)] + [whole] * 4,
+        out_specs=(whole, whole),
         scratch_shapes=[
             pltpu.VMEM((slots, tokens.shape[0]), BF16),
-            pltpu.VMEM((down.shape[1], width), BF16),
             *four,
             pltpu.VMEM((2, SIDE * SIDE, weight.shape[0], kv // 2), BF16),
             pltpu.VMEM((2, slots, kv // 2), F32),
-            pltpu.VMEM((slots, down.shape[1]), F32),
-            pltpu.VMEM((down.shape[1], width), F32),
+            pltpu.VMEM((slots, at.shape[0]), F32),
+            pltpu.VMEM((at.shape[0], width), F32),
             pltpu.VMEM(b.shape, F32),
-            pltpu.VMEM((down.shape[1], 128), F32),
-            pltpu.VMEM((2, 2, 2, 2, 2, 2, SLAB, 128), F32),
-            halves(CUT),
-            halves(SLAB - CUT),
+            pltpu.VMEM((at.shape[0], 128), F32),
+            slabs,
+            slabs,
+            slabs,
+            pltpu.VMEM((width // 128, 8, 128), F32),
+            pltpu.VMEM((8, 128), F32),
+            pltpu.VMEM((8, 128), F32),
+            tuple(chain(r) for r in ROUTES),
             dma((steps + 1,)),
             dma((steps + 1,)),
             dma((steps + 1,)),
@@ -454,14 +484,14 @@
             dma((PARTS,)),
             dma((PARTS, 16)),
             dma((2 * PARTS,)),
-            dma((14,)),
-            dma((14,)),
+            dma((SUM_SEMS,)),
+            dma((SUM_SEMS,)),
         ],
         compiler_params=pltpu.CompilerParams(
             collective_id=0, has_side_effects=True, vmem_limit_bytes=62 << 20
         ),
         name="exchange_and_adapt",
-    )(caps, count, bound, user, tokens, goals, weight, down, b)
+    )(caps, count, bound, user, tokens, goals, weight, at, b, noise_a, noise_b)
 
 
 def body(
@@ -477,17 +507,11 @@
     down_noise,
     up_noise,
 ):
-    myself = lax.axis_index(BOTH)
-    bound = clip_norm_bound[0]
-    slab = main(
-        user_row_cap, device_row_count, clip_norm_bound, row_owner_user, tokens, targets, value_weight,
-        adapter_down, adapter_up,
+    update_a, update_b = main(
+        user_row_cap, device_row_count, clip_norm_bound, row_owner_user.T, tokens, targets, value_weight,
+        adapter_down.T, adapter_up, down_noise, up_noise.T,
     )
-    odd = myself % 2
-    mine = jnp.where(odd == 0, slab[:, :64], slab[:, 64:])
-    update_a = mine[:ROWS_A].T + bound * down_noise
-    update_b = mine[ROWS_A:].T + bound * up_noise
-    return update_a, update_b
+    return update_a, update_b.T
 
 
 def solution(mesh):

time: 154 us -> 147 us (0.955)
  Pallas kernels: 145 us -> 142 us
  local copies, waits for them, and re-layouts: 4.99 us -> 2.65 us
    pallas_call x1, Pallas kernels: 145 us -> 142 us  [main(): pl.pallas_call(main_kernel, out_shape=tuple((jax.ShapeDtypeStruct(n.shape...]
    unnamed x8 -> x2, local copies, waits for them, and re-layouts: 4.99 us -> 2.65 us
where the time goes in v5:
time: 147 us; the launch traced here: 146 us
  Pallas kernels  142 us (97%)
  local copies, waits for them, and re-layouts  2.65 us (2%)
  between operations  1.93 us (1%)
    pallas_call x1, Pallas kernels, main(): pl.pallas_call(main_kernel, out_shape=tuple((jax.ShapeDtypeStruct(n.shape...  142 us

profile of v5, /device:TPU:0, one launch (start us, length us, event | category | flops | bytes accessed | tf_op | source)
XLA Modules:
  0.0 146.3 jit_solution(4122550097123366663)
XLA Ops:
  1.9 141.7 %exchange_and_adapt.1 = (f32[64,64]{1,0:T(8,128)}, f32[8,64]{1,0:T(8,128)}) custom-call(s32[128]{0:T(128)} %cap_ref.1, s32[1]{0:T(128)S(6)} %copy.15.count_ref, f32[1]{0:T(128)S(6)} %copy.16.bound_ref, s32[1,192]{1,0:T(1,128)} %bitcast.7, bf16[192,8192]{1,0:T(8,128)(2,1)} %tok_ref.1, bf16[192,1024]{1,0:T(8,128)(2,1)} %tgt_ref.1, bf16[512,1024]{1,0:T(8,128)(2,1)} %w_ref.1, ...), custom_call_target="tpu_custom_call" | custom-call | tf_op jit(solution)/shard_map/exchange_and_adapt/pallas_call | solution.py:457
  143.7 1.4 copy.17
  145.1 1.3 copy.18

commit v6 on v5

--- a/solution.py
+++ b/solution.py
@@ -143,8 +143,9 @@
 ROWS_F = 16
 ROWS_G = 32
 AHEAD = 2
-PARTS = 2
-PIECE = 256
+PARTS = ((0, 176), (176, 384))
+PLANES = 384
+QUARTER = 32
 ORDER = [(1, 0), (0, 1), (3, 0), (0, 3), (1, 1), (3, 3), (1, 3), (3, 1), (2, 0), (0, 2), (2, 1), (1, 2), (2, 3), (3, 2), (2, 2)]
 
 
@@ -163,7 +164,7 @@
 def main_kernel(
     cap_ref, count_ref, bound_ref, user_ref, tok_ref, tgt_ref, w_ref, at_ref, b_ref, na_ref, nb_ref,
     oa_ref, ob_ref, place_ref, st, sx, rt, rx, pt, px, gt, gx, wf, acc, hid, a1, bcur, sq,
-    given, kept, taken, packed, own_factor, far_factor, chains, fsend, frecv, gsend, grecv, wsend, wrecv, csend, crecv, local, ssend, srecv,
+    given, kept, taken, packed, own_factor, far_factor, chains, fsend, frecv, gsend, grecv, wsend, wrecv, ysend, yrecv, csend, crecv, local, ssend, srecv,
 ):
     y, c, x, z = places()
     g, f = y * 2 + c, x * SIDE + z
@@ -192,13 +193,9 @@
         pl.semaphore_signal(barrier, inc=1, device_id=(to, f), device_id_type=MESH)
 
     keep = []
-    for h in range(PARTS):
-        rows = slice(h * PIECE, (h + 1) * PIECE)
-        for n in range(2):
-            keep.append(
-                pltpu.make_async_copy(w_ref.at[rows, n * half : (n + 1) * half], wf.at[n, f, rows], local.at[2 * h + n])
-            )
-            keep[-1].start()
+    for n in range(2):
+        keep.append(pltpu.make_async_copy(w_ref.at[:, n * half : (n + 1) * half], wf.at[n, f], local.at[n]))
+        keep[-1].start()
 
     user = user_ref[...]
     per = user.shape[1]
@@ -262,39 +259,63 @@
         most = q.at[: slots - ROWS_G]
         pltpu.make_async_copy(most, most, grecv.at[k]).wait()
 
-    def weight(i, h):
-        return wf.at[c, column(piece(i, h, a, b), c), h * PIECE : (h + 1) * PIECE]
+    def send(src, dst, ssem, rsem, device):
+        pltpu.make_async_remote_copy(
+            src_ref=src, dst_ref=dst, send_sem=ssem, recv_sem=rsem, device_id=device, device_id_type=MESH
+        ).start()
+
+    def await_bytes(ref, sem):
+        pltpu.make_async_copy(ref, ref, sem).wait()
+
+    yn = sides(y, c)
+    beyond = sides(yn[1], c)[0]
+    my_half = pl.ds(pl.multiple_of(c * half, half), half)
+
+    def quarter(q):
+        return pl.ds(pl.multiple_of(PLANES + q * QUARTER, 16), QUARTER)
+
+    def col_of(i, h=0):
+        return column(piece(i, h, a, b), c)
 
     def pass_on(i, h):
-        level = i.bit_length()
-        to_ref = weight(i, h)
+        rows = slice(*PARTS[h])
+        ref = wf.at[c, col_of(i, h), rows]
+        src = ref
         if i == 0:
-            src = w_ref.at[h * PIECE : (h + 1) * PIECE, pl.ds(pl.multiple_of(c * half, half), half)]
+            src = w_ref.at[rows, my_half]
         else:
-            src = to_ref
-            pltpu.make_async_copy(src, src, wrecv.at[h, i]).wait()
-            swap(i, h)
+            await_bytes(ref, wrecv.at[h, i])
+        for n in range(i.bit_length(), 4):
+            send(src, ref, wsend.at[h], wrecv.at[h, (1 << n) + i], (g, col_of(1 << n, h)))
+
+    def pass_quarter(i, level):
+        ref = wf.at[c, col_of(i), quarter(y)]
+        src = ref
+        if level == 0:
+            src = w_ref.at[quarter(y), my_half]
+        else:
+            await_bytes(ref, yrecv.at[0, i])
         for n in range(level, 4):
-            to = column(piece(1 << n, h, a, b), c)
-            pltpu.make_async_remote_copy(
-                src_ref=src, dst_ref=to_ref, send_sem=wsend.at[h], recv_sem=wrecv.at[h, (1 << n) + i],
-                device_id=(g, to), device_id_type=MESH,
-            ).start()
-
-    def swap(i, h):
-        ref = weight(i, h)
-        pltpu.make_async_remote_copy(
-            src_ref=ref, dst_ref=ref, send_sem=csend.at[h], recv_sem=crecv.at[h, i],
-            device_id=(y * 2 + 1 - c, f), device_id_type=MESH,
-        ).start()
-
-    def other_column(i, h):
-        return column(piece(i, h, b, a), 1 - c)
-
-    def add(n, col, h):
-        per = chunk // (PARTS * PIECE)
-        x_cols = gx[col // per, :, pl.ds(pl.multiple_of(col % per * (PARTS * PIECE) + h * PIECE, PIECE), PIECE)]
-        acc[n] += mm(x_cols, wf[n, col, h * PIECE : (h + 1) * PIECE, :], 1, 0)
+            send(src, ref, ysend.at[0], yrecv.at[0, (1 << n) + i], (g, col_of(1 << n)))
+        if level:
+            for n in range(2):
+                send(ref, ref, ysend.at[1 + n], yrecv.at[1 + n, i], (yn[n] * 2 + c, f))
+
+    def relay(i):
+        ref = wf.at[c, col_of(i), quarter(yn[0])]
+        await_bytes(ref, yrecv.at[1, i])
+        send(ref, ref, ysend.at[3], yrecv.at[3, i], (yn[1] * 2 + c, f))
+
+    def add(n, col):
+        depth = w_ref.shape[0]
+        per = chunk // depth
+        x_cols = gx[col // per, :, pl.ds(pl.multiple_of(col % per * depth, depth), depth)]
+        acc[n] += mm(x_cols, wf[n, col], 1, 0)
+
+    def add_other(i):
+        col = column(piece(i, 0, b, a), 1 - c)
+        await_bytes(wf.at[1 - c, col], crecv.at[i])
+        add(1 - c, col)
 
     place_rows(0)
     pl.semaphore_wait(barrier, len(f_peers) + len(g_peers))
@@ -303,16 +324,36 @@
     start_f(1)
     acc[...] = jnp.zeros_like(acc)
     hid[...] = jnp.zeros_like(hid)
-    todo = {1: [0], 6: [1], 8: [2, 3], 10: [4, 5, 6, 7]}
+    both = range(len(PARTS))
+    def last_quarters():
+        @pl.loop(8, 16)
+        def _(i):
+            pass_quarter(i, 4)
+
+    def relays(lo, hi):
+        @pl.loop(lo, hi)
+        def _(i):
+            relay(i)
+
+    todo = {
+        1: lambda: pass_quarter(0, 0),
+        2: lambda: pass_quarter(1, 1),
+        3: lambda: [pass_quarter(i, 2) for i in (2, 3)],
+        4: lambda: [pass_quarter(i, 3) for i in (4, 5, 6, 7)],
+        5: lambda: [pass_on(0, h) for h in both] + [last_quarters()],
+        7: lambda: [pass_on(1, h) for h in both] + [relays(1, 8)],
+        8: lambda: [relays(8, 16)],
+        9: lambda: [pass_on(i, h) for i in (2, 3) for h in both],
+        10: lambda: [pass_on(i, h) for i in (4, 5, 6, 7) for h in both],
+    }
     for k in range(1, steps + 1 + AHEAD):
         if 1 < k <= steps:
             place_rows(k)
             start_f(k)
         if k >= AHEAD:
             turn_rows(k - AHEAD)
-        for i in todo.get(k, []):
-            for h in range(PARTS):
-                pass_on(i, h)
+        if k in todo:
+            todo[k]()
 
     end_g(0)
     for k in range(1, steps + 1):
@@ -321,33 +362,33 @@
     for d in keep:
         d.wait()
     for n in range(2):
-        for h in range(PARTS):
-            add(n, f, h)
-
-    @pl.loop(1, 8)
+        add(n, f)
+
+    @pl.loop(1, 16)
     def _(i):
-        for h in range(PARTS):
-            add(c, column(piece(i, h, a, b), c), h)
-            col = other_column(i, h)
-            ref = wf.at[1 - c, col, h * PIECE : (h + 1) * PIECE]
-            pltpu.make_async_copy(ref, ref, crecv.at[h, i]).wait()
-            add(1 - c, col, h)
-
-    @pl.loop(8, 16)
-    def _(i):
-        for h in range(PARTS):
-            ref = weight(i, h)
-            pltpu.make_async_copy(ref, ref, wrecv.at[h, i]).wait()
-            swap(i, h)
-            add(c, column(piece(i, h, a, b), c), h)
-
-    @pl.loop(8, 16)
-    def _(i):
-        for h in range(PARTS):
-            col = other_column(i, h)
-            ref = wf.at[1 - c, col, h * PIECE : (h + 1) * PIECE]
-            pltpu.make_async_copy(ref, ref, crecv.at[h, i]).wait()
-            add(1 - c, col, h)
+        col = col_of(i)
+        twin = i % 2 * 2 + i // 2 % 2 + i // 4 % 2 * 8 + i // 8 * 4
+
+        @pl.when(i >= 8)
+        def _():
+            await_bytes(wf.at[c, col, slice(*PARTS[0])], wrecv.at[0, i])
+
+        @pl.when(twin >= 8)
+        def _():
+            await_bytes(wf.at[c, col, slice(*PARTS[1])], wrecv.at[1, twin])
+
+        await_bytes(wf.at[c, col, quarter(yn[1])], yrecv.at[2, i])
+        await_bytes(wf.at[c, col, quarter(beyond)], yrecv.at[3, i])
+        shard = wf.at[c, col]
+        send(shard, shard, csend.at[0], crecv.at[i], (y * 2 + 1 - c, f))
+        add(c, col)
+
+        @pl.when(i >= 3)
+        def _():
+            add_other(i - 2)
+
+    add_other(14)
+    add_other(15)
 
     cap, bound = cap_ref[g * SIDE * SIDE + f].astype(F32), bound_ref[0]
     used = gt[:, kv:]
@@ -426,10 +467,11 @@
         pltpu.make_async_copy(most, most, fsend.at[k]).wait()
         most = p.at[: slots - ROWS_G]
         pltpu.make_async_copy(most, most, gsend.at[k]).wait()
-    for h in range(PARTS):
-        sent = wf.at[0, :15, h * PIECE : (h + 1) * PIECE]
-        pltpu.make_async_copy(sent, sent, wsend.at[h]).wait()
-        pltpu.make_async_copy(sent, sent, csend.at[h]).wait()
+    for h in both:
+        await_bytes(wf.at[0, :15, slice(*PARTS[h])], wsend.at[h])
+    for n in range(4):
+        await_bytes(wf.at[0, :15, :QUARTER], ysend.at[n])
+    await_bytes(wf.at[0, :15], csend.at[0])
 
 
 def main(caps, count, bound, user, tokens, goals, weight, at, b, noise_a, noise_b):
@@ -479,11 +521,13 @@
             dma((steps + 1,)),
             dma((steps + 1,)),
             dma((steps + 1,)),
-            dma((PARTS,)),
-            dma((PARTS, 16)),
-            dma((PARTS,)),
-            dma((PARTS, 16)),
-            dma((2 * PARTS,)),
+            dma((len(PARTS),)),
+            dma((len(PARTS), 16)),
+            dma((4,)),
+            dma((4, 16)),
+            dma((1,)),
+            dma((16,)),
+            dma((2,)),
             dma((SUM_SEMS,)),
             dma((SUM_SEMS,)),
         ],

time: 147 us -> 142 us (0.966)
  Pallas kernels: 142 us -> 138 us
    pallas_call x1, Pallas kernels: 142 us -> 138 us  [main(): pl.pallas_call(main_kernel, out_shape=tuple((jax.ShapeDtypeStruct(n.shape...]
where the time goes in v6:
time: 142 us
  Pallas kernels  138 us (97%)
  local copies, waits for them, and re-layouts  2.65 us (2%)
  between operations  1.93 us (1%)
    pallas_call x1, Pallas kernels, main(): pl.pallas_call(main_kernel, out_shape=tuple((jax.ShapeDtypeStruct(n.shape...  138 us

profile of v6, /device:TPU:0, one launch (start us, length us, event | category | flops | bytes accessed | tf_op | source)
XLA Modules:
  0.0 142.2 jit_solution(16392722549387606325)
XLA Ops:
  1.9 137.6 %exchange_and_adapt.1 = (f32[64,64]{1,0:T(8,128)}, f32[8,64]{1,0:T(8,128)}) custom-call(s32[128]{0:T(128)} %cap_ref.1, s32[1]{0:T(128)S(6)} %copy.15.count_ref, f32[1]{0:T(128)S(6)} %copy.16.bound_ref, s32[1,192]{1,0:T(1,128)} %bitcast.7, bf16[192,8192]{1,0:T(8,128)(2,1)} %tok_ref.1, bf16[192,1024]{1,0:T(8,128)(2,1)} %tgt_ref.1, bf16[512,1024]{1,0:T(8,128)(2,1)} %w_ref.1, ...), custom_call_target="tpu_custom_call" | custom-call | tf_op jit(solution)/shard_map/exchange_and_adapt/pallas_call | solution.py:499
  139.5 1.4 copy.17
  140.9 1.3 copy.18

commit v7 on v6

--- a/solution.py
+++ b/solution.py
@@ -48,19 +48,24 @@
 
 
 ROUTES = [
-    ("y1", "y2", "x1", "x2", "ring"),
-    ("x1", "x2", "y1", "y2", "ring"),
-    ("z", "y1", "y2", "x1", "x2", "pair"),
+    ("y1", "y2", "xz"),
+    ("x1", "x2", "yz"),
+    ("z", "y1", "block"),
 ]
+LAST = {
+    "xz": [(0, dx, dz) for dx in range(SIDE) for dz in range(SIDE)][1:],
+    "yz": [(dy, 0, dz) for dy in range(SIDE) for dz in range(SIDE)][1:],
+    "block": [(n, dx, m) for n in ("same", "second") for dx in range(SIDE) for m in ("same", "low")][1:],
+}
 THIRD = SLAB // len(ROUTES)
 FIRST_SEM = SIDE + 1
-SUM_SEMS = FIRST_SEM + sum(len(r) + 2 * ("ring" in r) for r in ROUTES)
+SUM_SEMS = FIRST_SEM + sum(len(LAST.get(dim, (0,))) for r in ROUTES for dim in r)
 
 
 def sum_slabs(kept, taken, factor, far, chains, send, recv):
     y, c, x, z = places()
 
-    def dev(y=y, c=c, x=x, z=z):
+    def dev(y=y, x=x, z=z):
         return (y * 2 + c, x * SIDE + z)
 
     yb, xb, yn, xn = bits(y, c), bits(x, c), sides(y, c), sides(x, c)
@@ -71,7 +76,6 @@
         "x1": dev(x=xn[0]),
         "x2": dev(x=xn[1]),
         "z": dev(z=mirror(z)),
-        "pair": dev(z=low(z)),
     }
     started = []
 
@@ -92,29 +96,30 @@
     def at(ref, left, dim, i):
         return ref.at[(slice(None),) * left.index(dim) + (i,)]
 
+    def slab_of(ref, left, y, x, z):
+        own = dict(zip(("y1", "y2", "x1", "x2", "z"), (*bits(y, c), *bits(x, c), z // 2)))
+        return ref.at[tuple(own[d] for d in left)]
+
     def launch(n, step):
-        route, bufs = ROUTES[n], chains[n]
-        dim, ref, left = route[step], now[n], dims[n]
-        into = bufs[step + 1]
-        if dim == "ring":
-            flying[n] = [
-                go(ref.at[(z + j) % SIDE // 2], into.at[j - 1], dev(z=(z + j) % SIDE)) for j in range(1, SIDE)
-            ]
-        elif dim == "pair":
-            flying[n] = [go(ref, into, to[dim])]
+        dim, ref, left = ROUTES[n][step], now[n], dims[n]
+        into = chains[n][step + 1]
+        if dim in LAST:
+            flying[n] = []
+            for k, (dy, dx, dz) in enumerate(LAST[dim]):
+                zz = z if dz == "same" else low(z) if dz == "low" else (z + dz) % SIDE
+                yy = y if dy == "same" else yn[1] if dy == "second" else (y + dy) % SIDE
+                xx = (x + dx) % SIDE
+                flying[n].append(go(slab_of(ref, left, yy, xx, zz), into.at[k], dev(yy, xx, zz)))
         else:
             flying[n] = [go(at(ref, left, dim, 1 - bit[dim]), into, to[dim])]
 
     def land(n, step):
-        route, bufs = ROUTES[n], chains[n]
-        dim, ref, left = route[step], now[n], dims[n]
-        into = bufs[step + 1]
+        dim, ref, left = ROUTES[n][step], now[n], dims[n]
+        into = chains[n][step + 1]
         for d in flying[n]:
             d.wait_recv()
-        if dim == "ring":
-            return ref[z // 2] + into[0] + into[1] + into[2]
-        if dim == "pair":
-            return ref[...] + into[...]
+        if dim in LAST:
+            return slab_of(ref, left, y, x, z)[...] + jnp.sum(into[...], axis=0)
         into[...] += at(ref, left, dim, bit[dim])[...]
         now[n] = into
         dims[n] = [v for v in left if v != dim]
@@ -123,9 +128,8 @@
     results = [None] * len(ROUTES)
     for n in range(len(ROUTES)):
         rows = slice(n * THIRD, (n + 1) * THIRD)
-        ref = chains[n][0]
-        ref[...] = near * kept[:, :, :, :, :, rows] + away * taken[:, :, :, :, :, rows]
-        now.append(ref)
+        chains[n][0][...] = near * kept[:, :, :, :, :, rows] + away * taken[:, :, :, :, :, rows]
+        now.append(chains[n][0])
         dims.append(["y1", "y2", "x1", "x2", "z"])
         flying.append(None)
         launch(n, 0)
@@ -162,7 +166,7 @@
 
 
 def main_kernel(
-    cap_ref, count_ref, bound_ref, user_ref, tok_ref, tgt_ref, w_ref, at_ref, b_ref, na_ref, nb_ref,
+    cap_ref, count_ref, bound_ref, user_ref, tok_ref, tgt_ref, w_ref, at_ref, b_ref,
     oa_ref, ob_ref, place_ref, st, sx, rt, rx, pt, px, gt, gx, wf, acc, hid, a1, bcur, sq,
     given, kept, taken, packed, own_factor, far_factor, chains, fsend, frecv, gsend, grecv, wsend, wrecv, ysend, yrecv, csend, crecv, local, ssend, srecv,
 ):
@@ -191,6 +195,10 @@
         pl.semaphore_signal(barrier, inc=1, device_id=(g, to), device_id_type=MESH)
     for to in g_peers:
         pl.semaphore_signal(barrier, inc=1, device_id=(to, f), device_id_type=MESH)
+    further = [((y + dy) % SIDE, x, (z + dz) % SIDE) for dy in range(1, SIDE) for dz in range(1, SIDE)]
+    further += [(sides(y, c)[1], (x + dx) % SIDE, zz) for dx in range(1, SIDE) for zz in (z, low(z))]
+    for ty, tx, tz in further:
+        pl.semaphore_signal(barrier, inc=1, device_id=(ty * 2 + c, tx * SIDE + tz), device_id_type=MESH)
 
     keep = []
     for n in range(2):
@@ -318,7 +326,7 @@
         add(1 - c, col)
 
     place_rows(0)
-    pl.semaphore_wait(barrier, len(f_peers) + len(g_peers))
+    pl.semaphore_wait(barrier, len(f_peers) + len(g_peers) + len(further))
     start_f(0)
     place_rows(1)
     start_f(1)
@@ -456,8 +464,8 @@
         d.wait_recv()
     slab = sum_slabs(kept, taken, own_factor[...], far_factor[...], chains, ssend, srecv)
     val = jnp.where(z % 2 == 1, slab[:, ROWS_A:], slab[:, :ROWS_A])
-    oa_ref[...] = val[:ROWS_A].T + bound * na_ref[...]
-    ob_ref[...] = val[ROWS_A:] + bound * nb_ref[...]
+    oa_ref[...] = val[:ROWS_A].T
+    ob_ref[...] = val[ROWS_A:]
     for d in first:
         d.wait_send()
 
@@ -474,7 +482,7 @@
     await_bytes(wf.at[0, :15], csend.at[0])
 
 
-def main(caps, count, bound, user, tokens, goals, weight, at, b, noise_a, noise_b):
+def main(caps, count, bound, user, tokens, goals, weight, at, b, outs):
     width, kv = tokens.shape[1], b.shape[1]
     slots = ROWS_F * SIDE * SIDE
     chunk = 1024
@@ -490,16 +498,15 @@
     def chain(route):
         left, bufs = 5, []
         for dim in ("start", *route):
-            if dim in ("y1", "y2", "x1", "x2", "z"):
-                left -= 1
-            lead = (SIDE - 1,) if dim == "ring" else (2,) * left
+            left -= dim not in LAST and dim != "start"
+            lead = (len(LAST[dim]),) if dim in LAST else (2,) * left
             bufs.append(pltpu.VMEM((*lead, THIRD, 128), F32))
         return tuple(bufs)
 
     return pl.pallas_call(
         main_kernel,
-        out_shape=tuple(jax.ShapeDtypeStruct(n.shape, F32) for n in (noise_a, noise_b)),
-        in_specs=[scalars] * 3 + [whole] * 3 + [pl.BlockSpec(memory_space=pl.ANY)] + [whole] * 4,
+        out_shape=tuple(jax.ShapeDtypeStruct(n.shape, F32) for n in outs),
+        in_specs=[scalars] * 3 + [whole] * 3 + [pl.BlockSpec(memory_space=pl.ANY)] + [whole] * 2,
         out_specs=(whole, whole),
         scratch_shapes=[
             pltpu.VMEM((slots, tokens.shape[0]), BF16),
@@ -535,7 +542,7 @@
             collective_id=0, has_side_effects=True, vmem_limit_bytes=62 << 20
         ),
         name="exchange_and_adapt",
-    )(caps, count, bound, user, tokens, goals, weight, at, b, noise_a, noise_b)
+    )(caps, count, bound, user, tokens, goals, weight, at, b)
 
 
 def body(
@@ -551,11 +558,12 @@
     down_noise,
     up_noise,
 ):
-    update_a, update_b = main(
+    sum_a, sum_b = main(
         user_row_cap, device_row_count, clip_norm_bound, row_owner_user.T, tokens, targets, value_weight,
-        adapter_down.T, adapter_up, down_noise, up_noise.T,
+        adapter_down.T, adapter_up, (down_noise, up_noise.T),
     )
-    return update_a, update_b.T
+    bound = clip_norm_bound[0]
+    return sum_a + bound * down_noise, sum_b.T + bound * up_noise
 
 
 def solution(mesh):

time: 142 us -> 138 us (0.972)
  Pallas kernels: 138 us -> 133 us
  other arithmetic: 0 us -> 2.66 us
  local copies, waits for them, and re-layouts: 2.65 us -> 0.01 us
    pallas_call x1, Pallas kernels: 138 us -> 133 us  [main(): pl.pallas_call(main_kernel, out_shape=tuple((jax.ShapeDtypeStruct(n.shape...]
    add x0 -> x2, other arithmetic: none -> 2.66 us  [body(): return (sum_a + bound * down_noise, sum_b.T + bound * up_noise)]
    unnamed x2 -> x4, local copies, waits for them, and re-layouts: 2.65 us -> 0.01 us
where the time goes in v7:
time: 138 us
  Pallas kernels  133 us (96%)
  other arithmetic  2.66 us (2%)
  between operations  1.97 us (1%)
    pallas_call x1, Pallas kernels, main(): pl.pallas_call(main_kernel, out_shape=tuple((jax.ShapeDtypeStruct(n.shape...  133 us

profile of v7, /device:TPU:0, one launch (start us, length us, event | category | flops | bytes accessed | tf_op | source)
XLA Modules:
  0.0 138.0 jit_solution(552086241557070613)
XLA Ops:
  0.6 0.0 copy-start.1
  0.6 0.0 copy-start
  2.0 133.4 %exchange_and_adapt.1 = (f32[64,64]{1,0:T(8,128)}, f32[8,64]{1,0:T(8,128)}) custom-call(s32[128]{0:T(128)} %cap_ref.1, s32[1]{0:T(128)S(6)} %copy.13.count_ref, f32[1]{0:T(128)} %copy.14.bound_ref, s32[1,192]{1,0:T(1,128)} %bitcast.8, bf16[192,8192]{1,0:T(8,128)(2,1)} %tok_ref.1, bf16[192,1024]{1,0:T(8,128)(2,1)} %tgt_ref.1, bf16[512,1024]{1,0:T(8,128)(2,1)} %w_ref.1, ...), custom_call_target="tpu_custom_call" | custom-call | tf_op jit(solution)/shard_map/exchange_and_adapt/pallas_call | solution.py:506
  135.4 0.0 copy-done
  135.4 1.4 %multiply_add_fusion = f32[64,64]{1,0:T(8,128)} fusion(f32[64,64]{1,0:T(8,128)} %get-tuple-element.4, f32[64,64]{1,0:T(8,128)S(1)} %copy-done, f32[]{:T(128)} %bitcast.5), kind=kLoop, calls=%fused_computation | loop fusion | flops 8192 | bytes 49156 | tf_op jit(solution)/shard_map/add | solution.py:566
  136.8 0.0 copy-done.1
  136.8 1.3 bitcast_add_fusion
Async XLA Ops:
  0.6 136.1 %copy-start.1 = (f32[64,8]{0,1:T(8,128)S(1)}, f32[64,8]{0,1:T(8,128)}, u32[]{:S(2)}) copy-start(f32[64,8]{0,1:T(8,128)} %param.21) | copy-start | bytes 6148
  0.6 134.7 %copy-start = (f32[64,64]{1,0:T(8,128)S(1)}, f32[64,64]{1,0:T(8,128)}, u32[]{:S(2)}) copy-start(f32[64,64]{1,0:T(8,128)} %param.20) | copy-start | bytes 49156

commit v8 on v7

--- a/solution.py
+++ b/solution.py
@@ -166,9 +166,9 @@
 
 
 def main_kernel(
-    cap_ref, count_ref, bound_ref, user_ref, tok_ref, tgt_ref, w_ref, at_ref, b_ref,
-    oa_ref, ob_ref, place_ref, st, sx, rt, rx, pt, px, gt, gx, wf, acc, hid, a1, bcur, sq,
-    given, kept, taken, packed, own_factor, far_factor, chains, fsend, frecv, gsend, grecv, wsend, wrecv, ysend, yrecv, csend, crecv, local, ssend, srecv,
+    cap_ref, count_ref, bound_ref, user_ref, tok_hbm, tgt_ref, w_ref, at_hbm, b_ref,
+    oa_ref, ob_ref, place_ref, tok_ref, at_ref, st, sx, rt, rx, pt, px, gt, gx, wf, acc, hid, a1, bcur, sq,
+    given, kept, taken, packed, own_factor, far_factor, chains, fsend, frecv, gsend, grecv, wsend, wrecv, ysend, yrecv, csend, crecv, local, loads, ssend, srecv,
 ):
     y, c, x, z = places()
     g, f = y * 2 + c, x * SIDE + z
@@ -199,6 +199,14 @@
     further += [(sides(y, c)[1], (x + dx) % SIDE, zz) for dx in range(1, SIDE) for zz in (z, low(z))]
     for ty, tx, tz in further:
         pl.semaphore_signal(barrier, inc=1, device_id=(ty * 2 + c, tx * SIDE + tz), device_id_type=MESH)
+
+    early = []
+    for k in range(steps):
+        cols = slice(k * chunk, (k + 1) * chunk)
+        early.append(pltpu.make_async_copy(tok_hbm.at[:, cols], tok_ref.at[:, cols], loads.at[k]))
+    early.append(pltpu.make_async_copy(at_hbm, at_ref, loads.at[steps]))
+    for d in early:
+        d.start()
 
     keep = []
     for n in range(2):
@@ -239,6 +247,7 @@
             s[:, :kv] = mm(place, tgt_ref[...], 1, 0).astype(BF16)
             s[:, kv:] = mm(place, flags, 1, 0).astype(BF16)
         else:
+            early[k - 1].wait()
             s[...] = mm(place, tok_ref[:, (k - 1) * chunk : k * chunk], 1, 0).astype(BF16)
 
     def start_f(k):
@@ -363,6 +372,7 @@
         if k in todo:
             todo[k]()
 
+    early[steps].wait()
     end_g(0)
     for k in range(1, steps + 1):
         end_g(k)
@@ -490,6 +500,7 @@
     extra = kv + 128
     whole = pl.BlockSpec(memory_space=pltpu.VMEM)
     scalars = pl.BlockSpec(memory_space=pltpu.SMEM)
+    left = pl.BlockSpec(memory_space=pl.ANY)
     four = [pltpu.VMEM((slots, extra), BF16), pltpu.VMEM((steps, slots, chunk), BF16)] * 4
     dma = pltpu.SemaphoreType.DMA
 
@@ -506,10 +517,12 @@
     return pl.pallas_call(
         main_kernel,
         out_shape=tuple(jax.ShapeDtypeStruct(n.shape, F32) for n in outs),
-        in_specs=[scalars] * 3 + [whole] * 3 + [pl.BlockSpec(memory_space=pl.ANY)] + [whole] * 2,
+        in_specs=[scalars] * 3 + [whole, left, whole, left, left, whole],
         out_specs=(whole, whole),
         scratch_shapes=[
             pltpu.VMEM((slots, tokens.shape[0]), BF16),
+            pltpu.VMEM(tokens.shape, BF16),
+            pltpu.VMEM(at.shape, BF16),
             *four,
             pltpu.VMEM((2, SIDE * SIDE, weight.shape[0], kv // 2), BF16),
             pltpu.VMEM((2, slots, kv // 2), F32),
@@ -535,6 +548,7 @@
             dma((1,)),
             dma((16,)),
             dma((2,)),
+            dma((steps + 1,)),
             dma((SUM_SEMS,)),
             dma((SUM_SEMS,)),
         ],

time: 138 us -> 137 us (level)
  no operation moved by 1% of the time
where the time goes in v8:
time: 137 us
  Pallas kernels  132 us (96%)
  other arithmetic  2.66 us (2%)
  between operations  1.97 us (1%)
    pallas_call x1, Pallas kernels, main(): pl.pallas_call(main_kernel, out_shape=tuple((jax.ShapeDtypeStruct(n.shape...  132 us

profile of v8, /device:TPU:0, one launch (start us, length us, event | category | flops | bytes accessed | tf_op | source)
XLA Modules:
  0.0 136.8 jit_solution(5534060104739427756)
XLA Ops:
  0.6 0.0 copy-start.1
  0.6 0.0 copy-start
  2.0 132.2 %exchange_and_adapt.1 = (f32[64,64]{1,0:T(8,128)}, f32[8,64]{1,0:T(8,128)}) custom-call(s32[128]{0:T(128)} %cap_ref.1, s32[1]{0:T(128)S(6)} %copy.13.count_ref, f32[1]{0:T(128)} %copy.14.bound_ref, s32[1,192]{1,0:T(1,128)} %bitcast.8, bf16[192,8192]{1,0:T(8,128)(2,1)} %tok_hbm.1, bf16[192,1024]{1,0:T(8,128)(2,1)} %tgt_ref.1, bf16[512,1024]{1,0:T(8,128)(2,1)} %w_ref.1, ...), custom_call_target="tpu_custom_call" | custom-call | tf_op jit(solution)/shard_map/exchange_and_adapt/pallas_call | solution.py:517
  134.2 0.0 copy-done
  134.2 1.4 %multiply_add_fusion = f32[64,64]{1,0:T(8,128)} fusion(f32[64,64]{1,0:T(8,128)} %get-tuple-element.4, f32[64,64]{1,0:T(8,128)S(1)} %copy-done, f32[]{:T(128)} %bitcast.5), kind=kLoop, calls=%fused_computation | loop fusion | flops 8192 | bytes 49156 | tf_op jit(solution)/shard_map/add | solution.py:580
  135.6 0.0 copy-done.1
  135.6 1.3 bitcast_add_fusion
Async XLA Ops:
  0.6 134.9 %copy-start.1 = (f32[64,8]{0,1:T(8,128)S(1)}, f32[64,8]{0,1:T(8,128)}, u32[]{:S(2)}) copy-start(f32[64,8]{0,1:T(8,128)} %param.21) | copy-start | bytes 6148
  0.6 133.5 %copy-start = (f32[64,64]{1,0:T(8,128)S(1)}, f32[64,64]{1,0:T(8,128)}, u32[]{:S(2)}) copy-start(f32[64,64]{1,0:T(8,128)} %param.20) | copy-start | bytes 49156

commit v9 on v8

--- a/solution.py
+++ b/solution.py
@@ -428,7 +428,7 @@
     bcur[...] = b0.astype(F32) - rate * grad_b
     hid[...] = jnp.zeros_like(hid)
 
-    @pl.loop(0, steps)
+    @pl.loop(0, steps, unroll=4)
     def _(k):
         rows = gx[k]
         now = at_ref[:, part(k)].astype(F32) - rate * (scale * mm(back, rows, 0, 0))

time: 137 us -> 136 us (level)
  no operation moved by 1% of the time
where the time goes in v9:
time: 136 us
  Pallas kernels  131 us (96%)
  other arithmetic  2.66 us (2%)
  between operations  1.97 us (1%)
    pallas_call x1, Pallas kernels, main(): pl.pallas_call(main_kernel, out_shape=tuple((jax.ShapeDtypeStruct(n.shape...  131 us

profile of v9, /device:TPU:0, one launch (start us, length us, event | category | flops | bytes accessed | tf_op | source)
XLA Modules:
  0.0 135.8 jit_solution(13080638754633812319)
XLA Ops:
  0.6 0.0 copy-start.1
  0.6 0.0 copy-start
  2.0 131.2 %exchange_and_adapt.1 = (f32[64,64]{1,0:T(8,128)}, f32[8,64]{1,0:T(8,128)}) custom-call(s32[128]{0:T(128)} %cap_ref.1, s32[1]{0:T(128)S(6)} %copy.13.count_ref, f32[1]{0:T(128)} %copy.14.bound_ref, s32[1,192]{1,0:T(1,128)} %bitcast.8, bf16[192,8192]{1,0:T(8,128)(2,1)} %tok_hbm.1, bf16[192,1024]{1,0:T(8,128)(2,1)} %tgt_ref.1, bf16[512,1024]{1,0:T(8,128)(2,1)} %w_ref.1, ...), custom_call_target="tpu_custom_call" | custom-call | tf_op jit(solution)/shard_map/exchange_and_adapt/pallas_call | solution.py:517
  133.1 0.0 copy-done
  133.1 1.4 %multiply_add_fusion = f32[64,64]{1,0:T(8,128)} fusion(f32[64,64]{1,0:T(8,128)} %get-tuple-element.4, f32[64,64]{1,0:T(8,128)S(1)} %copy-done, f32[]{:T(128)} %bitcast.5), kind=kLoop, calls=%fused_computation | loop fusion | flops 8192 | bytes 49156 | tf_op jit(solution)/shard_map/add | solution.py:580
  134.5 0.0 copy-done.1
  134.5 1.3 bitcast_add_fusion
Async XLA Ops:
  0.6 133.9 %copy-start.1 = (f32[64,8]{0,1:T(8,128)S(1)}, f32[64,8]{0,1:T(8,128)}, u32[]{:S(2)}) copy-start(f32[64,8]{0,1:T(8,128)} %param.21) | copy-start | bytes 6148
  0.6 132.5 %copy-start = (f32[64,64]{1,0:T(8,128)S(1)}, f32[64,64]{1,0:T(8,128)}, u32[]{:S(2)}) copy-start(f32[64,64]{1,0:T(8,128)} %param.20) | copy-start | bytes 49156
